TPU v7x, 128 devices: a whole 4x4x4 slice. The times are simulated.
128 devices in a mesh: dp: 8 (over z_hi, y), tensor: 4 (over z_lo, core), replica: 4 (over x).
Axes of the slice: x: 4, y: 4, z: 4 (z_hi: 2, z_lo: 2; z = z_hi * 2 + z_lo), core: 2. Of those that a mesh axis runs over, the one named last changes fastest.
Arguments:
- queries: bfloat16 [8192, 8192], P(('dp', 'replica'), 'tensor'), may hold values from -8 to 8
- d_out: bfloat16 [8192, 8192], P(('dp', 'replica'), 'tensor'), may hold values from -48 to 48
- conv_keys: bfloat16 [8192, 1024], P(('dp', 'replica'), 'tensor'), may hold values from -12 to 12
- conv_values: bfloat16 [8192, 1024], P(('dp', 'replica'), 'tensor'), may hold values from -6 to 6
- segment_ids: int32 [32, 256], P(('dp', 'replica')), may hold values from 0 to 3, never falling along the last dimension, each value on 1 to 192 neighbouring positions
- master_keys: float32 [4096, 1024], P('dp', 'tensor'), may hold values from -8 to 8
- master_values: float32 [4096, 1024], P('dp', 'tensor'), may hold values from -6 to 6
- moment_keys: float32 [4096, 1024], P('dp', 'tensor'), may hold values from -3 to 3
- moment_values: float32 [4096, 1024], P('dp', 'tensor'), may hold values from -3 to 3
- second_keys: float32 [4096, 1024], P('dp', 'tensor'), may hold values from 0.01 to 1
- second_values: float32 [4096, 1024], P('dp', 'tensor'), may hold values from 0.01 to 1
Outputs:
- new_master_keys: float32 [4096, 1024], P('dp', 'tensor')
- new_master_values: float32 [4096, 1024], P('dp', 'tensor')
- new_moment_keys: float32 [4096, 1024], P('dp', 'tensor')
- new_moment_values: float32 [4096, 1024], P('dp', 'tensor')
- new_second_keys: float32 [4096, 1024], P('dp', 'tensor')
- new_second_values: float32 [4096, 1024], P('dp', 'tensor')
- served_keys: bfloat16 [4096, 1024], P(None, 'tensor')
- served_values: bfloat16 [4096, 1024], P(None, 'tensor')
- grad_keys: float32 [4096, 1024], P('dp', 'tensor')
- grad_values: float32 [4096, 1024], P('dp', 'tensor')
Inputs may be any that keep to these rules, and one draw needn't show every extreme that they name: `segment_ids`: each row holds the conversation numbers of one device's 256 tokens.
All inputs are finite; a program needn't handle non-finite values.
Results may differ from a plain program's by a relative error of at most 0.0065.
Values may be sent and summed in bfloat16 or wider, within the bound.
No kernel may reach another device: no remote copies, remote signals or barrier semaphores. Data moves between devices by JAX's collectives and lax.ppermute only.
A program may use at most 256 MiB of HBM per device.

v0:
```python
import functools

import jax
import jax.numpy as jnp
from jax import lax
from jax.experimental import pallas as pl
from jax.experimental.pallas import tpu as pltpu
from jax.sharding import PartitionSpec as P


Q_HEADS = 64
KV_HEADS = 8
HEAD = 128
GROUP = Q_HEADS // KV_HEADS
TOK = 256
STEP = 20
BETA_ONE = 0.9
BETA_TWO = 0.95
LEARN_RATE = 0.05
WEIGHT_DECAY = 0.1
EPSILON = 1e-08
SCALE = HEAD**-0.5
LOG2E = 1.4426950408889634
NT = (((1,), (1,)), ((), ()))
F32 = jnp.float32
BF16 = jnp.bfloat16


OFFSETS = ((0, 0), (0, 1), (0, 3), (0, 2), (1, 0), (1, 1), (1, 3), (1, 2))


def block_rows(share, absolute):
    if absolute:
        return [b * share for b in range(8)]
    me = lax.axis_index("dp")
    far, mine = lax.div(me, 4), lax.rem(me, 4)
    return [(lax.rem(far + z, 2) * 4 + lax.rem(mine + y, 4)) * share for z, y in OFFSETS]


def quarter_rows(size):
    here = lax.axis_index("replica")
    return [lax.rem(here + j, 4) * size for j in range(4)]


def attend_kernel(hp, ck, pieces, absolute, seg_ref, q_ref, do_ref, ko_ref, vo_ref, *refs):
    count = 1 + max(p[0] for p in pieces)
    arrays, refs = refs[:count], refs[count:]
    sends, refs = refs[:5], refs[5:]
    k_ref, v_ref, s_ref, p_ref, dp_ref, dk_acc, dv_acc, sems = refs
    keys = k_ref.shape[0]
    rows = hp * TOK
    steps = GROUP // hp
    chunks = keys // ck
    c = SCALE * LOG2E

    starts = block_rows(keys // 8, absolute)
    loads = [[], []]
    for side, dst in enumerate((k_ref, v_ref)):
        for n, (array, src, size, block, low) in enumerate(pieces):
            at = pl.multiple_of(starts[block] + low, size)
            load = pltpu.make_async_copy(
                arrays[array].at[pl.ds(src, size), pl.ds(side * HEAD, HEAD)],
                dst.at[pl.ds(at, size), :],
                sems.at[side * len(pieces) + n],
            )
            load.start()
            loads[side].append(load)

    def cols(ref, step):
        parts = []
        for j in range(hp):
            at = (step * hp + j) * HEAD
            parts.append(ref[:, pl.ds(pl.multiple_of(at, HEAD), HEAD)])
        return jnp.concatenate(parts, axis=0)

    def fold(x):
        return x.reshape(x.shape[0] // 8, 8, rows)

    seg_row = jnp.broadcast_to(seg_ref[...].astype(F32), (TOK, TOK))
    u = lax.broadcasted_iota(jnp.int32, (TOK, TOK), 0)
    t = lax.broadcasted_iota(jnp.int32, (TOK, TOK), 1)
    seen = (seg_row == seg_row.T) & (u <= t)

    def spread(x, op):
        return jnp.broadcast_to(op(x, axis=0, keepdims=True), x.shape)

    def tick(at, one, two, three, state):
        highest, total, centred = state
        init = []
        if one:
            q1 = cols(q_ref, at)
            own = lax.dot_general(ko_ref[...], q1, NT, preferred_element_type=F32)
            parts = [jnp.where(seen, own[:, j * TOK : (j + 1) * TOK], -jnp.inf) for j in range(hp)]
            own = jnp.concatenate(parts, axis=1)
            init.append(jnp.max(fold(own), axis=0))
        if two:
            mc = spread(highest, jnp.max) * c
            q2, d2 = cols(q_ref, at - 1), cols(do_ref, at - 1)
            own2 = lax.dot_general(ko_ref[...], q2, NT, preferred_element_type=F32)
            parts = [jnp.where(seen, own2[:, j * TOK : (j + 1) * TOK], -jnp.inf) for j in range(hp)]
            own2 = jnp.concatenate(parts, axis=1)
            own_p = jnp.exp2(fold(own2) * c - mc[None])
            own_dp = fold(lax.dot_general(vo_ref[...], d2, NT, preferred_element_type=F32))
            init.append(jnp.sum(own_p, axis=0))
            init.append(jnp.sum(own_p * own_dp, axis=0))
        if three:
            inv = 1.0 / spread(total, jnp.sum)
            centre = spread(centred, jnp.sum) * inv
            q3, d3 = cols(q_ref, at - 2), cols(do_ref, at - 2)

        def body(i, carry):
            out = []
            here = pl.ds(pl.multiple_of(i * ck, ck), ck)
            if three:
                p = fold(p_ref[here, :]) * inv[None]
                ds = p * (fold(dp_ref[here, :]) - centre[None])
                p = p.reshape(ck, rows).astype(BF16)
                ds = ds.reshape(ck, rows).astype(BF16)
                dv_acc[here, :] += jnp.dot(p, d3, preferred_element_type=F32)
                dk_acc[here, :] += jnp.dot(ds, q3, preferred_element_type=F32)
            n = int(one)
            if two:
                p = jnp.exp2(fold(s_ref[here, :]) * c - mc[None])
                dp = lax.dot_general(v_ref[here, :], d2, NT, preferred_element_type=F32)
                total_now = carry[n] + jnp.sum(p, axis=0)
                centred_now = carry[n + 1] + jnp.sum(p * fold(dp), axis=0)
                p_ref[here, :] = p.reshape(ck, rows)
                dp_ref[here, :] = dp
            if one:
                s = lax.dot_general(k_ref[here, :], q1, NT, preferred_element_type=F32)
                s_ref[here, :] = s
                out.append(jnp.maximum(carry[0], jnp.max(fold(s), axis=0)))
            else:
                out.append(highest)
            if two:
                out += [total_now, centred_now]
            else:
                out += [total, centred]
            return tuple(out)

        full = (init[0] if one else highest,) + (tuple(init[int(one) :]) if two else (total, centred))

        def step(i, carry):
            picked = ([carry[0]] if one else []) + (list(carry[1:]) if two else [])
            return body(i, picked)

        return lax.fori_loop(0, chunks, step, full)

    none = jnp.zeros((8, rows), F32)
    state = (none, none, none)
    for load in loads[0]:
        load.wait()
    state = tick(0, True, False, False, state)
    dk_acc[...] = jnp.zeros_like(dk_acc)
    dv_acc[...] = jnp.zeros_like(dv_acc)
    for load in loads[1]:
        load.wait()
    state = tick(1, True, True, False, state)
    state = lax.fori_loop(2, steps, lambda at, st: tick(at, True, True, True, st), state)
    state = tick(steps, False, True, True, state)
    tick(steps + 1, False, False, True, state)
    send_keys, send_values = sends[0], sends[1:]
    blocks, _, size, _ = send_keys.shape
    turns = quarter_rows(size)
    for j in range(4):
        for block in range(blocks):
            here = pl.ds(pl.multiple_of(block * 4 * size + turns[j], size), size)
            send_keys[block, j] = (dk_acc[here, :] * SCALE).astype(BF16)
            send_values[j][block] = dv_acc[here, :].astype(BF16)


def attend(group, absolute, seg, queries, d_out, conv_keys, conv_values, arrays, pieces, hp=2, ck=2048):
    keys = sum(p[2] for p in pieces)
    rows = hp * TOK
    anywhere = pl.BlockSpec(memory_space=pltpu.HBM)
    wide = pl.BlockSpec((TOK, GROUP * HEAD), lambda i: (0, group))
    slim = pl.BlockSpec((TOK, HEAD), lambda i: (0, group))
    return pl.pallas_call(
        functools.partial(attend_kernel, hp, ck, pieces, absolute),
        grid=(1,),
        out_shape=[
            jax.ShapeDtypeStruct((8, 4, keys // 32, HEAD), BF16),
            *[jax.ShapeDtypeStruct((8, keys // 32, HEAD), BF16)] * 4,
        ],
        in_specs=[pl.BlockSpec((1, TOK), lambda i: (0, 0)), wide, wide, slim, slim]
        + [anywhere] * len(arrays),
        out_specs=[
            pl.BlockSpec((8, 4, keys // 32, HEAD), lambda i: (0, 0, 0, 0)),
            *[pl.BlockSpec((8, keys // 32, HEAD), lambda i: (0, 0, 0))] * 4,
        ],
        scratch_shapes=[pltpu.VMEM((keys, HEAD), BF16)] * 2
        + [pltpu.VMEM((keys, rows), F32)] * 3
        + [pltpu.VMEM((keys, HEAD), F32)] * 2
        + [pltpu.SemaphoreType.DMA((2 * len(pieces),))],
        cost_estimate=pl.CostEstimate(
            flops=8 * GROUP * TOK * keys * HEAD,
            bytes_accessed=8 << 20,
            transcendentals=GROUP * TOK * keys,
        ),
        compiler_params=pltpu.CompilerParams(vmem_limit_bytes=56 << 20),
        name="attend",
    )(seg, queries, d_out, conv_keys, conv_values, *arrays)


def fetch(value, offset):
    z, y = offset
    pairs = [(s, ((s // 4 + z) % 2) * 4 + (s % 4 - y) % 4) for s in range(8)]
    return lax.ppermute(value, "dp", pairs)


def relay_gather(own):
    half = own.shape[0] // 2
    far = fetch(own, (1, 0))
    up, down = fetch(own, (0, 1)), fetch(own, (0, 3))
    up, down, far = lax.optimization_barrier((up, down, far))
    from_far = fetch(jnp.concatenate([up[half:], down[half:]]), (1, 0))
    from_up = fetch(jnp.concatenate([up[:half], far[:half]]), (0, 1))
    from_down = fetch(jnp.concatenate([down[half:], far[:half]]), (0, 3))
    from_up, from_down, from_far = lax.optimization_barrier((from_up, from_down, from_far))
    last_far = fetch(from_down[:half], (1, 0))
    last_up = fetch(from_up[half:], (0, 1))
    return own, up, down, far, from_up, from_down, from_far, last_up, last_far


def relay_pieces(share):
    half = share // 2
    whole = [(0, 0, share, 0, 0), (1, 0, share, 1, 0), (2, 0, share, 2, 0), (3, 0, share, 4, 0)]
    halves = [
        (4, 0, half, 3, 0),
        (4, half, half, 5, 0),
        (5, 0, half, 3, half),
        (5, half, half, 6, 0),
        (6, 0, half, 5, half),
        (6, half, half, 6, half),
        (7, 0, half, 7, 0),
        (8, 0, half, 7, half),
    ]
    return whole + halves


def turn(value, by):
    return lax.ppermute(value, "replica", [(s, (s + by) % 4) for s in range(4)])


def total(parts):
    parts = [p.astype(F32) for p in parts]
    while len(parts) > 1:
        parts = [a + b for a, b in zip(parts[::2], parts[1::2])]
    return parts[0]


def dp_sum(parts):
    got = lax.all_to_all(parts, "dp", 0, 0, tiled=True)
    return total([got[i] for i in range(8)])


def replica_sum(parts):
    return total([parts[0]] + [turn(parts[j], j) for j in (1, 3, 2)])


def adamw_step(param, moment, second, grad):
    moment_new = BETA_ONE * moment + (1.0 - BETA_ONE) * grad
    second_new = BETA_TWO * second + (1.0 - BETA_TWO) * grad * grad
    moment_hat = moment_new / (1.0 - BETA_ONE**STEP)
    second_hat = second_new / (1.0 - BETA_TWO**STEP)
    param_new = param - LEARN_RATE * (
        moment_hat / (jnp.sqrt(second_hat) + EPSILON) + WEIGHT_DECAY * param
    )
    return (param_new, moment_new, second_new)


def place_kernel(pieces, skip, *refs):
    count = 1 + max(p[0] for p in pieces)
    arrays, refs = refs[:count], refs[count + skip :]
    keys_ref, values_ref, hold, sems_in, sems_out = refs
    half = keys_ref.shape[1]
    starts = block_rows(keys_ref.shape[0] // 8, False)
    loads, at = [], 0
    for n, (array, src, size, _, _) in enumerate(pieces):
        load = pltpu.make_async_copy(
            arrays[array].at[pl.ds(src, size), :], hold.at[pl.ds(at, size), :], sems_in.at[n]
        )
        load.start()
        loads.append((load, at))
        at += size
    stores = []
    for n, (_, _, size, block, low) in enumerate(pieces):
        load, at = loads[n]
        load.wait()
        to = pl.multiple_of(starts[block] + low, size)
        for side, out in enumerate((keys_ref, values_ref)):
            store = pltpu.make_async_copy(
                hold.at[pl.ds(at, size), pl.ds(side * half, half)],
                out.at[pl.ds(to, size), :],
                sems_out.at[2 * n + side],
            )
            store.start()
            stores.append(store)
    for store in stores:
        store.wait()


def place(arrays, pieces, keys, started=()):
    rows, wide = sum(p[2] for p in pieces), arrays[0].shape[1]
    out = jax.ShapeDtypeStruct((keys, wide // 2), BF16)
    anywhere = pl.BlockSpec(memory_space=pltpu.HBM)
    first = len(arrays)
    return pl.pallas_call(
        functools.partial(place_kernel, pieces, len(started)),
        out_shape=[out, out],
        in_specs=[anywhere] * (len(arrays) + len(started)),
        out_specs=[anywhere] * 2,
        input_output_aliases={first + i: i for i in range(len(started))},
        scratch_shapes=[
            pltpu.VMEM((rows, wide), BF16),
            pltpu.SemaphoreType.DMA((len(pieces),)),
            pltpu.SemaphoreType.DMA((2 * len(pieces),)),
        ],
        name="place",
    )(*arrays, *started)


def update_kernel(serve, *refs):
    grads, olds, outs = refs[:4], refs[4:10], refs[10:]
    size = grads[0].shape[0]
    half = grads[0].shape[1] // 2
    turns = quarter_rows(size)
    for j in range(4):
        at = pl.ds(pl.multiple_of(turns[j], size), size)
        for side in range(2):
            cols = slice(side * half, (side + 1) * half)
            grad = grads[j][:, cols].astype(F32)
            new = adamw_step(*[olds[2 * n + side][at, :] for n in range(3)], grad)
            if serve:
                outs[0][at, cols] = new[0].astype(BF16)
            else:
                for n in range(3):
                    outs[2 * n + side][at, :] = new[n]
                outs[6 + side][at, :] = grad


def update(serve, grads, olds):
    share, half = olds[0].shape
    vm = pl.BlockSpec(memory_space=pltpu.VMEM)
    shard = jax.ShapeDtypeStruct((share, half), F32)
    served = jax.ShapeDtypeStruct((share, 2 * half), BF16)
    outs = [served] if serve else [shard] * 8
    return pl.pallas_call(
        functools.partial(update_kernel, serve),
        out_shape=outs,
        in_specs=[vm] * 10,
        out_specs=[vm] * len(outs),
        cost_estimate=pl.CostEstimate(flops=0, bytes_accessed=8 << 20, transcendentals=0),
        name="serve" if serve else "update",
    )(*grads, *olds)


def per_device(
    queries,
    d_out,
    conv_keys,
    conv_values,
    segment_ids,
    master_keys,
    master_values,
    moment_keys,
    moment_values,
    second_keys,
    second_values,
):
    share = master_keys.shape[0]
    relayed = relay_pieces(share)

    def own_block(head):
        at = slice(head * HEAD, (head + 1) * HEAD)
        return jnp.concatenate([master_keys[:, at], master_values[:, at]], axis=1).astype(BF16)

    def attention(group, absolute, arrays, pieces):
        tokens = (segment_ids, queries, d_out, conv_keys, conv_values)
        return attend(group, absolute, *tokens, arrays, pieces)

    later = jnp.broadcast_to(own_block(1), (8, share, 2 * HEAD))
    first = relay_gather(own_block(0))
    *first, later = lax.optimization_barrier((*first, later))
    parts_first = attention(0, False, first, relayed)
    second = lax.all_to_all(later, "dp", 0, 0, tiled=True).reshape(8 * share, 2 * HEAD)
    parts_second = attention(
        1, True, [second], [(0, b * share, share, b, 0) for b in range(8)]
    )
    keys_sum = [dp_sum(parts[0]) for parts in (parts_first, parts_second)]
    values_sum = [replica_sum(parts_first[1:])]
    values_sum.append(replica_sum(parts_second[1:]))
    keys_low = jnp.concatenate(keys_sum, axis=2).astype(BF16)
    values_low = jnp.concatenate(values_sum, axis=2).astype(BF16)
    keys_quarter = replica_sum([keys_low[j] for j in range(4)])
    values_quarter = dp_sum(values_low)
    both = jnp.concatenate([keys_quarter, values_quarter], axis=1).astype(BF16)
    grads = [both] + [turn(both, -j) for j in (1, 2, 3)]
    olds = (master_keys, master_values, moment_keys, moment_values, second_keys, second_values)
    (served,) = update(True, grads, olds)
    *news, grad_keys, grad_values = update(False, grads, olds)
    arrays = relay_gather(served)
    started = ()
    for low, high in ((0, 4), (4, 7), (7, 9)):
        part = [(p[0] - low, *p[1:]) for p in relayed if low <= p[0] < high]
        started = place(arrays[low:high], part, 8 * share, started)
    return (*news, *started, grad_keys, grad_values)


def solution(mesh):
    tokens = P(("dp", "replica"), "tensor")
    shard = P("dp", "tensor")
    served = P(None, "tensor")
    return jax.shard_map(
        per_device,
        mesh=mesh,
        in_specs=(tokens,) * 4 + (P(("dp", "replica"), None),) + (shard,) * 6,
        out_specs=(shard,) * 6 + (served,) * 2 + (shard,) * 2,
        check_vma=False,
    )
```

profile of v0, /device:TPU:0, one launch (start us, length us, event | category | flops | bytes accessed | tf_op | source)
XLA Modules:
  0.0 216.1 jit_solution(7710562257125411290)
XLA Ops:
  2.9 3.2 %collective-permute-start = (bf16[512,256]{1,0:T(8,128)(2,1)S(1)}, bf16[512,256]{1,0:T(8,128)(2,1)S(1)}, u32[]{:S(2)}, u32[]{:S(2)}) collective-permute-start(bf16[512,256]{1,0:T(8,128)(2,1)S(1)} %pad_maximum_fusion.6.refs_0_), channel_id=1, source_target_pairs={{0,48},{16,0},{32,16},{48,32},{64,112},{80,64},{96,80},{112,96},{1... | collective-permute-start | bytes 786440 | tf_op jit(solution)/shard_map/ppermute | solution.py:208
  6.1 3.9 %collective-permute-start.2 = (bf16[512,256]{1,0:T(8,128)(2,1)S(1)}, bf16[512,256]{1,0:T(8,128)(2,1)S(1)}, u32[]{:S(2)}, u32[]{:S(2)}) collective-permute-start(bf16[512,256]{1,0:T(8,128)(2,1)S(1)} %pad_maximum_fusion.6.refs_0_), channel_id=1, source_target_pairs={{0,64},{16,80},{32,96},{48,112},{64,0},{80,16},{96,32},{112,48},{1... | collective-permute-start | bytes 786440 | tf_op jit(solution)/shard_map/ppermute | solution.py:208
  10.0 1.7 collective-permute-done.refs_1_
  11.7 3.4 %collective-permute-done.1.refs_2_ = bf16[512,256]{1,0:T(8,128)(2,1)S(1)} collective-permute-done((bf16[512,256]{1,0:T(8,128)(2,1)S(1)}, bf16[512,256]{1,0:T(8,128)(2,1)S(1)}, u32[]{:S(2)}, u32[]{:S(2)}) %collective-permute-start.1) | collective-permute-done | bytes 262176 | tf_op jit(solution)/shard_map/ppermute | solution.py:208
  16.2 3.0 %collective-permute-start.3 = (bf16[512,256]{1,0:T(8,128)(2,1)S(1)}, bf16[512,256]{1,0:T(8,128)(2,1)S(1)}, u32[]{:S(2)}, u32[]{:S(2)}) collective-permute-start(bf16[512,256]{1,0:T(8,128)(2,1)S(1)} %get-tuple-element.118), channel_id=1, source_target_pairs={{0,48},{16,0},{32,16},{48,32},{64,112},{80,64},{96,80},{112,96},{1... | collective-permute-start | bytes 786440 | tf_op jit(solution)/shard_map/ppermute | solution.py:208
  19.2 3.2 %collective-permute-start.5 = (bf16[512,256]{1,0:T(8,128)(2,1)S(1)}, bf16[512,256]{1,0:T(8,128)(2,1)}, u32[]{:S(2)}, u32[]{:S(2)}) collective-permute-start(bf16[512,256]{1,0:T(8,128)(2,1)S(1)} %get-tuple-element.116), channel_id=1, source_target_pairs={{0,64},{16,80},{32,96},{48,112},{64,0},{80,16},{96,32},{112,48},{1... | collective-permute-start | bytes 786440 | tf_op jit(solution)/shard_map/ppermute | solution.py:208
  22.4 1.2 collective-permute-done.3.refs_4_
  23.6 3.4 %collective-permute-done.4.refs_5_ = bf16[512,256]{1,0:T(8,128)(2,1)S(1)} collective-permute-done((bf16[512,256]{1,0:T(8,128)(2,1)S(1)}, bf16[512,256]{1,0:T(8,128)(2,1)S(1)}, u32[]{:S(2)}, u32[]{:S(2)}) %collective-permute-start.4) | collective-permute-done | bytes 262176 | tf_op jit(solution)/shard_map/ppermute | solution.py:208
  27.4 3.0 %collective-permute-start.6 = (bf16[256,256]{1,0:T(8,128)(2,1)S(1)}, bf16[256,256]{1,0:T(8,128)(2,1)S(1)}, u32[]{:S(2)}, u32[]{:S(2)}) collective-permute-start(bf16[256,256]{1,0:T(8,128)(2,1)S(1)} %slice.146), channel_id=1, source_target_pairs={{0,48},{16,0},{32,16},{48,32},{64,112},{80,64},{96,80},{112,96},{1... | collective-permute-start | bytes 393224 | tf_op jit(solution)/shard_map/ppermute | solution.py:208
  30.5 3.3 %collective-permute-start.7 = (bf16[256,256]{1,0:T(8,128)(2,1)S(1)}, bf16[256,256]{1,0:T(8,128)(2,1)S(1)}, u32[]{:S(2)}, u32[]{:S(2)}) collective-permute-start(bf16[256,256]{1,0:T(8,128)(2,1)S(1)} %slice.147), channel_id=1, source_target_pairs={{0,64},{16,80},{32,96},{48,112},{64,0},{80,16},{96,32},{112,48},{1... | collective-permute-start | bytes 393224 | tf_op jit(solution)/shard_map/ppermute | solution.py:208
  33.9 3.2 %collective-permute-done.7.refs_8_ = bf16[256,256]{1,0:T(8,128)(2,1)S(1)} collective-permute-done((bf16[256,256]{1,0:T(8,128)(2,1)S(1)}, bf16[256,256]{1,0:T(8,128)(2,1)S(1)}, u32[]{:S(2)}, u32[]{:S(2)}) %collective-permute-start.7) | collective-permute-done | bytes 131104 | tf_op jit(solution)/shard_map/ppermute | solution.py:208
  37.1 1.5 broadcast_in_dim.3
  38.6 4.5 %all-to-all-start.1 = ((bf16[8,512,256]{2,1,0:T(8,128)(2,1)}), bf16[8,512,256]{2,1,0:T(8,128)(2,1)S(1)}, u32[]{:S(2)}, u32[]{:S(2)}) async-start(bf16[8,512,256]{2,1,0:T(8,128)(2,1)} %broadcast_in_dim.3), calls=%async_computation.1 | async-start | bytes 4194304 | tf_op jit(solution)/shard_map/all_to_all | solution.py:386
  43.1 27.6 %attend.2 = (bf16[8,4,128,128]{3,2,1,0:T(8,128)(2,1)}, bf16[8,128,128]{2,1,0:T(8,128)(2,1)}, bf16[8,128,128]{2,1,0:T(8,128)(2,1)}, bf16[8,128,128]{2,1,0:T(8,128)(2,1)}, bf16[8,128,128]{2,1,0:T(8,128)(2,1)}) custom-call(s32[1,256]{1,0:T(1,128)} %seg_ref.3, bf16[256,2048]{1,0:T(8,128)(2,1)} %q_ref.3, bf16[256,2048]{1,0:T(8,128)(2,1)} %do_ref.3, ...), custom_call_target="tpu_custom_call" | custom-call | flops 8589934592 | bytes 8388608 | tf_op jit(solution)/shard_map/attend/pallas_call | solution.py:178
  70.7 7.2 %all-to-all-start = ((bf16[8,4,128,128]{3,2,1,0:T(8,128)(2,1)}), bf16[8,4,128,128]{3,2,1,0:T(8,128)(2,1)S(1)}, u32[]{:S(2)}, u32[]{:S(2)}) async-start(bf16[8,4,128,128]{3,2,1,0:T(8,128)(2,1)} %get-tuple-element.71), calls=%async_computation | async-start | bytes 2097152 | tf_op jit(solution)/shard_map/all_to_all | solution.py:253
  77.9 27.5 %attend.3 = (bf16[8,4,128,128]{3,2,1,0:T(8,128)(2,1)}, bf16[8,128,128]{2,1,0:T(8,128)(2,1)}, bf16[8,128,128]{2,1,0:T(8,128)(2,1)}, bf16[8,128,128]{2,1,0:T(8,128)(2,1)}, bf16[8,128,128]{2,1,0:T(8,128)(2,1)}) custom-call(s32[1,256]{1,0:T(1,128)} %seg_ref.3, bf16[256,2048]{1,0:T(8,128)(2,1)} %q_ref.3, bf16[256,2048]{1,0:T(8,128)(2,1)} %do_ref.3, ...), custom_call_target="tpu_custom_call" | custom-call | flops 8589934592 | bytes 8388608 | tf_op jit(solution)/shard_map/attend/pallas_call | solution.py:178
  105.5 7.3 %all-to-all-start.2 = ((bf16[8,4,128,128]{3,2,1,0:T(8,128)(2,1)}), bf16[8,4,128,128]{3,2,1,0:T(8,128)(2,1)S(1)}, u32[]{:S(2)}, u32[]{:S(2)}) async-start(bf16[8,4,128,128]{3,2,1,0:T(8,128)(2,1)} %get-tuple-element.73), calls=%async_computation.2 | async-start | bytes 2097152 | tf_op jit(solution)/shard_map/all_to_all | solution.py:253
  112.8 1.5 collective-permute-start.11
  114.3 1.7 collective-permute-start.12
  116.1 1.8 collective-permute-start.13
  118.5 2.7 %collective-permute-start.15 = (bf16[8,128,128]{2,1,0:T(8,128)(2,1)}, bf16[8,128,128]{2,1,0:T(8,128)(2,1)S(1)}, u32[]{:S(2)}, u32[]{:S(2)}) collective-permute-start(bf16[8,128,128]{2,1,0:T(8,128)(2,1)} %get-tuple-element.80), channel_id=1, source_target_pairs={{0,3},{1,0},{2,1},{3,2},{4,7},{5,4},{6,5},{7,6},{8,11},{9,8},{10,9... | collective-permute-start | bytes 786440 | tf_op jit(solution)/shard_map/ppermute | solution.py:242
  121.1 3.2 %collective-permute-done.11 = bf16[8,128,128]{2,1,0:T(8,128)(2,1)S(1)} collective-permute-done((bf16[8,128,128]{2,1,0:T(8,128)(2,1)}, bf16[8,128,128]{2,1,0:T(8,128)(2,1)S(1)}, u32[]{:S(2)}, u32[]{:S(2)}) %collective-permute-start.11) | collective-permute-done | bytes 262176 | tf_op jit(solution)/shard_map/ppermute | solution.py:242
  125.2 3.6 %collective-permute-done.13 = bf16[8,128,128]{2,1,0:T(8,128)(2,1)S(1)} collective-permute-done((bf16[8,128,128]{2,1,0:T(8,128)(2,1)S(1)}, bf16[8,128,128]{2,1,0:T(8,128)(2,1)S(1)}, u32[]{:S(2)}, u32[]{:S(2)}) %collective-permute-start.13) | collective-permute-done | bytes 262176 | tf_op jit(solution)/shard_map/ppermute | solution.py:242
  128.9 2.5 %collective-permute-done.14 = bf16[8,128,128]{2,1,0:T(8,128)(2,1)S(1)} collective-permute-done((bf16[8,128,128]{2,1,0:T(8,128)(2,1)}, bf16[8,128,128]{2,1,0:T(8,128)(2,1)S(1)}, u32[]{:S(2)}, u32[]{:S(2)}) %collective-permute-start.14) | collective-permute-done | bytes 262176 | tf_op jit(solution)/shard_map/ppermute | solution.py:242
  131.4 2.9 %collective-permute-done.16 = bf16[8,128,128]{2,1,0:T(8,128)(2,1)S(1)} collective-permute-done((bf16[8,128,128]{2,1,0:T(8,128)(2,1)S(1)}, bf16[8,128,128]{2,1,0:T(8,128)(2,1)S(1)}, u32[]{:S(2)}, u32[]{:S(2)}) %collective-permute-start.16) | collective-permute-done | bytes 262176 | tf_op jit(solution)/shard_map/ppermute | solution.py:242
  135.3 6.9 %all-to-all-start.3 = ((bf16[8,128,256]{2,1,0:T(8,128)(2,1)}), bf16[8,128,256]{2,1,0:T(8,128)(2,1)S(1)}, u32[]{:S(2)}, u32[]{:S(2)}) async-start(bf16[8,128,256]{2,1,0:T(8,128)(2,1)} %pad_maximum_fusion.2), calls=%async_computation.3 | async-start | bytes 1048576 | tf_op jit(solution)/shard_map/all_to_all | solution.py:253
  143.5 1.7 collective-permute-start.8
  145.2 1.5 collective-permute-start.9
  146.7 5.7 %all-to-all-done.3 = bf16[8,128,256]{2,1,0:T(8,128)(2,1)S(1)} async-done(((bf16[8,128,256]{2,1,0:T(8,128)(2,1)}), bf16[8,128,256]{2,1,0:T(8,128)(2,1)S(1)}, u32[]{:S(2)}, u32[]{:S(2)}) %all-to-all-start.3) | async-done | bytes 524320 | tf_op jit(solution)/shard_map/all_to_all | solution.py:253
  152.6 1.8 collective-permute-start.17
  154.4 1.3 collective-permute-start.18
  155.7 2.0 collective-permute-done.17.refs_1_
  157.7 3.2 %collective-permute-done.18.refs_2_ = bf16[128,512]{1,0:T(8,128)(2,1)S(1)} collective-permute-done((bf16[128,512]{1,0:T(8,128)(2,1)S(1)}, bf16[128,512]{1,0:T(8,128)(2,1)S(1)}, u32[]{:S(2)}, u32[]{:S(2)}) %collective-permute-start.18) | collective-permute-done | bytes 131104 | tf_op jit(solution)/shard_map/ppermute | solution.py:242
  160.9 1.4 collective-permute-done.19.refs_3_
  162.9 3.7 %serve.1.refs_0_ = bf16[512,512]{1,0:T(8,128)(2,1)} custom-call(bf16[128,512]{1,0:T(8,128)(2,1)} %copy-done.2, bf16[128,512]{1,0:T(8,128)(2,1)} %copy-done.7, bf16[128,512]{1,0:T(8,128)(2,1)} %copy-done.8, bf16[128,512]{1,0:T(8,128)(2,1)} %copy-done.9, f32[512,256]{1,0:T(8,128)} %refs_4_.3, f32[512,256]{1,0:T(8,128)} %refs_5_.3, f32[512,256]{1,0:T(8,128)} %refs_6_.3, ...), custom_call_target="tpu_custom_call" | custom-call | bytes 8388608 | tf_op jit(solution)/shard_map/serve/pallas_call | solution.py:348
  166.6 1.2 collective-permute-start.20
  168.7 2.1 collective-permute-start.22
  170.8 9.8 %collective-permute-done.20.refs_1_ = bf16[512,512]{1,0:T(8,128)(2,1)S(1)} collective-permute-done((bf16[512,512]{1,0:T(8,128)(2,1)}, bf16[512,512]{1,0:T(8,128)(2,1)S(1)}, u32[]{:S(2)}, u32[]{:S(2)}) %collective-permute-start.20) | collective-permute-done | bytes 524320 | tf_op jit(solution)/shard_map/ppermute | solution.py:208
  181.6 2.0 collective-permute-done.22.refs_3_
  184.4 1.8 collective-permute-start.23
  186.4 3.1 %collective-permute-start.25 = (bf16[512,512]{1,0:T(8,128)(2,1)S(1)}, bf16[512,512]{1,0:T(8,128)(2,1)S(1)}, u32[]{:S(2)}, u32[]{:S(2)}) collective-permute-start(bf16[512,512]{1,0:T(8,128)(2,1)S(1)} %get-tuple-element.104), channel_id=1, source_target_pairs={{0,64},{16,80},{32,96},{48,112},{64,0},{80,16},{96,32},{112,48},{1... | collective-permute-start | bytes 1572872 | tf_op jit(solution)/shard_map/ppermute | solution.py:208
  189.6 6.5 %collective-permute-done.23.refs_0_ = bf16[512,512]{1,0:T(8,128)(2,1)S(1)} collective-permute-done((bf16[512,512]{1,0:T(8,128)(2,1)S(1)}, bf16[512,512]{1,0:T(8,128)(2,1)S(1)}, u32[]{:S(2)}, u32[]{:S(2)}) %collective-permute-start.23) | collective-permute-done | bytes 524320 | tf_op jit(solution)/shard_map/ppermute | solution.py:208
  196.6 3.2 %collective-permute-done.25.refs_2_ = bf16[512,512]{1,0:T(8,128)(2,1)S(1)} collective-permute-done((bf16[512,512]{1,0:T(8,128)(2,1)S(1)}, bf16[512,512]{1,0:T(8,128)(2,1)S(1)}, u32[]{:S(2)}, u32[]{:S(2)}) %collective-permute-start.25) | collective-permute-done | bytes 524320 | tf_op jit(solution)/shard_map/ppermute | solution.py:208
  200.3 3.4 %collective-permute-start.27 = (bf16[256,512]{1,0:T(8,128)(2,1)S(1)}, bf16[256,512]{1,0:T(8,128)(2,1)S(1)}, u32[]{:S(2)}, u32[]{:S(2)}) collective-permute-start(bf16[256,512]{1,0:T(8,128)(2,1)S(1)} %slice.183), channel_id=1, source_target_pairs={{0,64},{16,80},{32,96},{48,112},{64,0},{80,16},{96,32},{112,48},{1... | collective-permute-start | bytes 786440 | tf_op jit(solution)/shard_map/ppermute | solution.py:208
  203.7 4.8 %update.1 = (f32[512,256]{1,0:T(8,128)}, f32[512,256]{1,0:T(8,128)}, f32[512,256]{1,0:T(8,128)}, f32[512,256]{1,0:T(8,128)}, f32[512,256]{1,0:T(8,128)}, /*index...) custom-call(bf16[128,512]{1,0:T(8,128)(2,1)} %copy-done.2, bf16[128,512]{1,0:T(8,128)(2,1)} %copy-done.7, ...), custom_call_target="tpu_custom_call" | custom-call | bytes 8388608 | tf_op jit(solution)/shard_map/update/pallas_call | solution.py:348
  208.5 2.5 %place.3 = (bf16[4096,256]{1,0:T(8,128)(2,1)}, bf16[4096,256]{1,0:T(8,128)(2,1)}) custom-call(bf16[512,512]{1,0:T(8,128)(2,1)} %serve.1.refs_0_, bf16[512,512]{1,0:T(8,128)(2,1)} %copy-done.1, bf16[512,512]{1,0:T(8,128)(2,1)} %copy-done.3, bf16[512,512]{1,0:T(8,128)(2,1)} %copy-done.4), custom_call_target="tpu_custom_call" | custom-call | tf_op jit(solution)/shard_map/place/pallas_call | solution.py:308
  211.0 2.2 %place.4 = (bf16[4096,256]{1,0:T(8,128)(2,1)}, bf16[4096,256]{1,0:T(8,128)(2,1)}) custom-call(bf16[512,512]{1,0:T(8,128)(2,1)} %copy-done.5, bf16[512,512]{1,0:T(8,128)(2,1)} %copy-done.6, bf16[512,512]{1,0:T(8,128)(2,1)} %copy-done.10, bf16[4096,256]{1,0:T(8,128)(2,1)} %get-tuple-element.94.refs_3_, ...), custom_call_target="tpu_custom_call", output_to_operand_aliasing={{0}: (3, {}), {1}: (4, {})} | custom-call | tf_op jit(solution)/shard_map/place/pallas_call | solution.py:308
  214.1 1.8 place.5
  (102 shorter events, 13.0 us)
Async XLA Ops:
  2.9 35.6 %copy-start.15 = (bf16[512,256]{1,0:T(8,128)(2,1)}, bf16[512,256]{1,0:T(8,128)(2,1)S(1)}, u32[]{:S(2)}) copy-start(bf16[512,256]{1,0:T(8,128)(2,1)S(1)} %pad_maximum_fusion.6.refs_0_) | copy-start | bytes 786436
  2.9 8.8 %collective-permute-start = (bf16[512,256]{1,0:T(8,128)(2,1)S(1)}, bf16[512,256]{1,0:T(8,128)(2,1)S(1)}, u32[]{:S(2)}, u32[]{:S(2)}) collective-permute-start(bf16[512,256]{1,0:T(8,128)(2,1)S(1)} %pad_maximum_fusion.6.refs_0_), channel_id=1, source_target_pairs={{0,48},{16,0},{32,16},{48,32},{64,112},{80,64},{96,80},{112,96},{1... | collective-permute-start | bytes 786440 | tf_op jit(solution)/shard_map/ppermute | solution.py:208
  6.1 9.0 %collective-permute-start.1 = (bf16[512,256]{1,0:T(8,128)(2,1)S(1)}, bf16[512,256]{1,0:T(8,128)(2,1)S(1)}, u32[]{:S(2)}, u32[]{:S(2)}) collective-permute-start(bf16[512,256]{1,0:T(8,128)(2,1)S(1)} %pad_maximum_fusion.6.refs_0_), channel_id=1, source_target_pairs={{0,16},{16,32},{32,48},{48,0},{64,80},{80,96},{96,112},{112,64},{1... | collective-permute-start | bytes 786440 | tf_op jit(solution)/shard_map/ppermute | solution.py:208
  6.1 9.9 %collective-permute-start.2 = (bf16[512,256]{1,0:T(8,128)(2,1)S(1)}, bf16[512,256]{1,0:T(8,128)(2,1)S(1)}, u32[]{:S(2)}, u32[]{:S(2)}) collective-permute-start(bf16[512,256]{1,0:T(8,128)(2,1)S(1)} %pad_maximum_fusion.6.refs_0_), channel_id=1, source_target_pairs={{0,64},{16,80},{32,96},{48,112},{64,0},{80,16},{96,32},{112,48},{1... | collective-permute-start | bytes 786440 | tf_op jit(solution)/shard_map/ppermute | solution.py:208
  11.7 26.8 %copy-start.16 = (bf16[512,256]{1,0:T(8,128)(2,1)}, bf16[512,256]{1,0:T(8,128)(2,1)S(1)}, u32[]{:S(2)}) copy-start(bf16[512,256]{1,0:T(8,128)(2,1)S(1)} %collective-permute-done.refs_1_) | copy-start | bytes 786436
  15.1 23.4 %copy-start.17 = (bf16[512,256]{1,0:T(8,128)(2,1)}, bf16[512,256]{1,0:T(8,128)(2,1)S(1)}, u32[]{:S(2)}) copy-start(bf16[512,256]{1,0:T(8,128)(2,1)S(1)} %collective-permute-done.1.refs_2_) | copy-start | bytes 786436
  16.0 22.5 %copy-start.18 = (bf16[512,256]{1,0:T(8,128)(2,1)}, bf16[512,256]{1,0:T(8,128)(2,1)S(1)}, u32[]{:S(2)}) copy-start(bf16[512,256]{1,0:T(8,128)(2,1)S(1)} %collective-permute-done.2.refs_3_) | copy-start | bytes 786436
  16.2 7.5 %collective-permute-start.3 = (bf16[512,256]{1,0:T(8,128)(2,1)S(1)}, bf16[512,256]{1,0:T(8,128)(2,1)S(1)}, u32[]{:S(2)}, u32[]{:S(2)}) collective-permute-start(bf16[512,256]{1,0:T(8,128)(2,1)S(1)} %get-tuple-element.118), channel_id=1, source_target_pairs={{0,48},{16,0},{32,16},{48,32},{64,112},{80,64},{96,80},{112,96},{1... | collective-permute-start | bytes 786440 | tf_op jit(solution)/shard_map/ppermute | solution.py:208
  19.2 7.8 %collective-permute-start.4 = (bf16[512,256]{1,0:T(8,128)(2,1)S(1)}, bf16[512,256]{1,0:T(8,128)(2,1)S(1)}, u32[]{:S(2)}, u32[]{:S(2)}) collective-permute-start(bf16[512,256]{1,0:T(8,128)(2,1)S(1)} %get-tuple-element.117), channel_id=1, source_target_pairs={{0,16},{16,32},{32,48},{48,0},{64,80},{80,96},{96,112},{112,64},{1... | collective-permute-start | bytes 786440 | tf_op jit(solution)/shard_map/ppermute | solution.py:208
  19.2 8.2 %collective-permute-start.5 = (bf16[512,256]{1,0:T(8,128)(2,1)S(1)}, bf16[512,256]{1,0:T(8,128)(2,1)}, u32[]{:S(2)}, u32[]{:S(2)}) collective-permute-start(bf16[512,256]{1,0:T(8,128)(2,1)S(1)} %get-tuple-element.116), channel_id=1, source_target_pairs={{0,64},{16,80},{32,96},{48,112},{64,0},{80,16},{96,32},{112,48},{1... | collective-permute-start | bytes 786440 | tf_op jit(solution)/shard_map/ppermute | solution.py:208
  23.6 14.9 %copy-start.19 = (bf16[512,256]{1,0:T(8,128)(2,1)}, bf16[512,256]{1,0:T(8,128)(2,1)S(1)}, u32[]{:S(2)}) copy-start(bf16[512,256]{1,0:T(8,128)(2,1)S(1)} %collective-permute-done.3.refs_4_) | copy-start | bytes 786436
  27.0 11.5 %copy-start.20 = (bf16[512,256]{1,0:T(8,128)(2,1)}, bf16[512,256]{1,0:T(8,128)(2,1)S(1)}, u32[]{:S(2)}) copy-start(bf16[512,256]{1,0:T(8,128)(2,1)S(1)} %collective-permute-done.4.refs_5_) | copy-start | bytes 786436
  27.4 6.4 %collective-permute-start.6 = (bf16[256,256]{1,0:T(8,128)(2,1)S(1)}, bf16[256,256]{1,0:T(8,128)(2,1)S(1)}, u32[]{:S(2)}, u32[]{:S(2)}) collective-permute-start(bf16[256,256]{1,0:T(8,128)(2,1)S(1)} %slice.146), channel_id=1, source_target_pairs={{0,48},{16,0},{32,16},{48,32},{64,112},{80,64},{96,80},{112,96},{1... | collective-permute-start | bytes 393224 | tf_op jit(solution)/shard_map/ppermute | solution.py:208
  30.5 6.6 %collective-permute-start.7 = (bf16[256,256]{1,0:T(8,128)(2,1)S(1)}, bf16[256,256]{1,0:T(8,128)(2,1)S(1)}, u32[]{:S(2)}, u32[]{:S(2)}) collective-permute-start(bf16[256,256]{1,0:T(8,128)(2,1)S(1)} %slice.147), channel_id=1, source_target_pairs={{0,64},{16,80},{32,96},{48,112},{64,0},{80,16},{96,32},{112,48},{1... | collective-permute-start | bytes 393224 | tf_op jit(solution)/shard_map/ppermute | solution.py:208
  38.6 32.1 %all-to-all-start.1 = ((bf16[8,512,256]{2,1,0:T(8,128)(2,1)}), bf16[8,512,256]{2,1,0:T(8,128)(2,1)S(1)}, u32[]{:S(2)}, u32[]{:S(2)}) async-start(bf16[8,512,256]{2,1,0:T(8,128)(2,1)} %broadcast_in_dim.3), calls=%async_computation.1 | async-start | bytes 4194304 | tf_op jit(solution)/shard_map/all_to_all | solution.py:386
  70.7 7.2 %copy-start = (bf16[8,512,256]{2,1,0:T(8,128)(2,1)}, bf16[8,512,256]{2,1,0:T(8,128)(2,1)S(1)}, u32[]{:S(2)}) copy-start(bf16[8,512,256]{2,1,0:T(8,128)(2,1)S(1)} %all-to-all-done.1) | copy-start | bytes 6291460
  70.7 34.8 %all-to-all-start = ((bf16[8,4,128,128]{3,2,1,0:T(8,128)(2,1)}), bf16[8,4,128,128]{3,2,1,0:T(8,128)(2,1)S(1)}, u32[]{:S(2)}, u32[]{:S(2)}) async-start(bf16[8,4,128,128]{3,2,1,0:T(8,128)(2,1)} %get-tuple-element.71), calls=%async_computation | async-start | bytes 2097152 | tf_op jit(solution)/shard_map/all_to_all | solution.py:253
  105.4 8.9 %copy-start.22 = (bf16[8,128,128]{2,1,0:T(8,128)(2,1)S(1)}, bf16[8,128,128]{2,1,0:T(8,128)(2,1)}, u32[]{:S(2)}) copy-start(bf16[8,128,128]{2,1,0:T(8,128)(2,1)} %get-tuple-element.76) | copy-start | bytes 786436
  105.4 10.6 %copy-start.21 = (bf16[8,128,128]{2,1,0:T(8,128)(2,1)S(1)}, bf16[8,128,128]{2,1,0:T(8,128)(2,1)}, u32[]{:S(2)}) copy-start(bf16[8,128,128]{2,1,0:T(8,128)(2,1)} %get-tuple-element.77) | copy-start | bytes 786436
  105.4 18.9 %copy-start.23 = (bf16[8,128,128]{2,1,0:T(8,128)(2,1)S(1)}, bf16[8,128,128]{2,1,0:T(8,128)(2,1)}, u32[]{:S(2)}) copy-start(bf16[8,128,128]{2,1,0:T(8,128)(2,1)} %get-tuple-element.81) | copy-start | bytes 786436
  105.4 23.3 %copy-start.11 = (bf16[8,128,128]{2,1,0:T(8,128)(2,1)S(1)}, bf16[8,128,128]{2,1,0:T(8,128)(2,1)}, u32[]{:S(2)}) copy-start(bf16[8,128,128]{2,1,0:T(8,128)(2,1)} %get-tuple-element.74) | copy-start | bytes 786436
  105.5 28.8 %copy-start.12 = (bf16[8,128,128]{2,1,0:T(8,128)(2,1)S(1)}, bf16[8,128,128]{2,1,0:T(8,128)(2,1)}, u32[]{:S(2)}) copy-start(bf16[8,128,128]{2,1,0:T(8,128)(2,1)} %get-tuple-element.78) | copy-start | bytes 786436
  105.5 29.8 %all-to-all-start.2 = ((bf16[8,4,128,128]{3,2,1,0:T(8,128)(2,1)}), bf16[8,4,128,128]{3,2,1,0:T(8,128)(2,1)S(1)}, u32[]{:S(2)}, u32[]{:S(2)}) async-start(bf16[8,4,128,128]{3,2,1,0:T(8,128)(2,1)} %get-tuple-element.73), calls=%async_computation.2 | async-start | bytes 2097152 | tf_op jit(solution)/shard_map/all_to_all | solution.py:253
  112.8 11.5 %collective-permute-start.11 = (bf16[8,128,128]{2,1,0:T(8,128)(2,1)}, bf16[8,128,128]{2,1,0:T(8,128)(2,1)S(1)}, u32[]{:S(2)}, u32[]{:S(2)}) collective-permute-start(bf16[8,128,128]{2,1,0:T(8,128)(2,1)} %get-tuple-element.75), channel_id=1, source_target_pairs={{0,1},{1,2},{2,3},{3,0},{4,5},{5,6},{6,7},{7,4},{8,9},{9,10},{10,1... | collective-permute-start | bytes 786440 | tf_op jit(solution)/shard_map/ppermute | solution.py:242
  114.3 10.8 %collective-permute-start.12 = (bf16[8,128,128]{2,1,0:T(8,128)(2,1)S(1)}, bf16[8,128,128]{2,1,0:T(8,128)(2,1)S(1)}, u32[]{:S(2)}, u32[]{:S(2)}) collective-permute-start(bf16[8,128,128]{2,1,0:T(8,128)(2,1)S(1)} %copy-done.22), channel_id=1, source_target_pairs={{0,3},{1,0},{2,1},{3,2},{4,7},{5,4},{6,5},{7,6},{8,11},{9,8},{10,9... | collective-permute-start | bytes 786440 | tf_op jit(solution)/shard_map/ppermute | solution.py:242
  116.1 12.7 %collective-permute-start.13 = (bf16[8,128,128]{2,1,0:T(8,128)(2,1)S(1)}, bf16[8,128,128]{2,1,0:T(8,128)(2,1)S(1)}, u32[]{:S(2)}, u32[]{:S(2)}) collective-permute-start(bf16[8,128,128]{2,1,0:T(8,128)(2,1)S(1)} %copy-done.21), channel_id=1, source_target_pairs={{0,2},{1,3},{2,0},{3,1},{4,6},{5,7},{6,4},{7,5},{8,10},{9,11},{10,... | collective-permute-start | bytes 786440 | tf_op jit(solution)/shard_map/ppermute | solution.py:242
  117.9 13.5 %collective-permute-start.14 = (bf16[8,128,128]{2,1,0:T(8,128)(2,1)}, bf16[8,128,128]{2,1,0:T(8,128)(2,1)S(1)}, u32[]{:S(2)}, u32[]{:S(2)}) collective-permute-start(bf16[8,128,128]{2,1,0:T(8,128)(2,1)} %get-tuple-element.79), channel_id=1, source_target_pairs={{0,1},{1,2},{2,3},{3,0},{4,5},{5,6},{6,7},{7,4},{8,9},{9,10},{10,1... | collective-permute-start | bytes 786440 | tf_op jit(solution)/shard_map/ppermute | solution.py:242
  118.5 12.9 %collective-permute-start.15 = (bf16[8,128,128]{2,1,0:T(8,128)(2,1)}, bf16[8,128,128]{2,1,0:T(8,128)(2,1)S(1)}, u32[]{:S(2)}, u32[]{:S(2)}) collective-permute-start(bf16[8,128,128]{2,1,0:T(8,128)(2,1)} %get-tuple-element.80), channel_id=1, source_target_pairs={{0,3},{1,0},{2,1},{3,2},{4,7},{5,4},{6,5},{7,6},{8,11},{9,8},{10,9... | collective-permute-start | bytes 786440 | tf_op jit(solution)/shard_map/ppermute | solution.py:242
  124.3 10.0 %collective-permute-start.16 = (bf16[8,128,128]{2,1,0:T(8,128)(2,1)S(1)}, bf16[8,128,128]{2,1,0:T(8,128)(2,1)S(1)}, u32[]{:S(2)}, u32[]{:S(2)}) collective-permute-start(bf16[8,128,128]{2,1,0:T(8,128)(2,1)S(1)} %copy-done.23), channel_id=1, source_target_pairs={{0,2},{1,3},{2,0},{3,1},{4,6},{5,7},{6,4},{7,5},{8,10},{9,11},{10,... | collective-permute-start | bytes 786440 | tf_op jit(solution)/shard_map/ppermute | solution.py:242
  135.3 17.1 %all-to-all-start.3 = ((bf16[8,128,256]{2,1,0:T(8,128)(2,1)}), bf16[8,128,256]{2,1,0:T(8,128)(2,1)S(1)}, u32[]{:S(2)}, u32[]{:S(2)}) async-start(bf16[8,128,256]{2,1,0:T(8,128)(2,1)} %pad_maximum_fusion.2), calls=%async_computation.3 | async-start | bytes 1048576 | tf_op jit(solution)/shard_map/all_to_all | solution.py:253
  142.6 9.9 %collective-permute-start.10 = (bf16[128,256]{1,0:T(8,128)(2,1)S(1)}, bf16[128,256]{1,0:T(8,128)(2,1)S(1)}, u32[]{:S(2)}, u32[]{:S(2)}) collective-permute-start(bf16[128,256]{1,0:T(8,128)(2,1)S(1)} %get-tuple-element.108), channel_id=1, source_target_pairs={{0,2},{1,3},{2,0},{3,1},{4,6},{5,7},{6,4},{7,5},{8,10},{9,11},{10,... | collective-permute-start | bytes 196616 | tf_op jit(solution)/shard_map/ppermute | solution.py:242
  143.5 9.1 %collective-permute-start.8 = (bf16[128,256]{1,0:T(8,128)(2,1)S(1)}, bf16[128,256]{1,0:T(8,128)(2,1)S(1)}, u32[]{:S(2)}, u32[]{:S(2)}) collective-permute-start(bf16[128,256]{1,0:T(8,128)(2,1)S(1)} %get-tuple-element.107), channel_id=1, source_target_pairs={{0,1},{1,2},{2,3},{3,0},{4,5},{5,6},{6,7},{7,4},{8,9},{9,10},{10,1... | collective-permute-start | bytes 196616 | tf_op jit(solution)/shard_map/ppermute | solution.py:242
  145.2 7.3 %collective-permute-start.9 = (bf16[128,256]{1,0:T(8,128)(2,1)S(1)}, bf16[128,256]{1,0:T(8,128)(2,1)S(1)}, u32[]{:S(2)}, u32[]{:S(2)}) collective-permute-start(bf16[128,256]{1,0:T(8,128)(2,1)S(1)} %get-tuple-element.109), channel_id=1, source_target_pairs={{0,3},{1,0},{2,1},{3,2},{4,7},{5,4},{6,5},{7,6},{8,11},{9,8},{10,9... | collective-permute-start | bytes 196616 | tf_op jit(solution)/shard_map/ppermute | solution.py:242
  152.6 9.6 %copy-start.2 = (bf16[128,512]{1,0:T(8,128)(2,1)}, bf16[128,512]{1,0:T(8,128)(2,1)S(1)}, u32[]{:S(2)}) copy-start(bf16[128,512]{1,0:T(8,128)(2,1)S(1)} %pad_maximum_fusion.9.refs_0_) | copy-start | bytes 393220
  152.6 5.0 %collective-permute-start.17 = (bf16[128,512]{1,0:T(8,128)(2,1)S(1)}, bf16[128,512]{1,0:T(8,128)(2,1)S(1)}, u32[]{:S(2)}, u32[]{:S(2)}) collective-permute-start(bf16[128,512]{1,0:T(8,128)(2,1)S(1)} %pad_maximum_fusion.9.refs_0_), channel_id=1, source_target_pairs={{0,3},{1,0},{2,1},{3,2},{4,7},{5,4},{6,5},{7,6},{8,11},{9,8},{10,9... | collective-permute-start | bytes 393224 | tf_op jit(solution)/shard_map/ppermute | solution.py:242
  154.4 6.5 %collective-permute-start.18 = (bf16[128,512]{1,0:T(8,128)(2,1)S(1)}, bf16[128,512]{1,0:T(8,128)(2,1)S(1)}, u32[]{:S(2)}, u32[]{:S(2)}) collective-permute-start(bf16[128,512]{1,0:T(8,128)(2,1)S(1)} %pad_maximum_fusion.9.refs_0_), channel_id=1, source_target_pairs={{0,2},{1,3},{2,0},{3,1},{4,6},{5,7},{6,4},{7,5},{8,10},{9,11},{10,... | collective-permute-start | bytes 393224 | tf_op jit(solution)/shard_map/ppermute | solution.py:242
  155.7 6.6 %collective-permute-start.19 = (bf16[128,512]{1,0:T(8,128)(2,1)S(1)}, bf16[128,512]{1,0:T(8,128)(2,1)S(1)}, u32[]{:S(2)}, u32[]{:S(2)}) collective-permute-start(bf16[128,512]{1,0:T(8,128)(2,1)S(1)} %pad_maximum_fusion.9.refs_0_), channel_id=1, source_target_pairs={{0,1},{1,2},{2,3},{3,0},{4,5},{5,6},{6,7},{7,4},{8,9},{9,10},{10,1... | collective-permute-start | bytes 393224 | tf_op jit(solution)/shard_map/ppermute | solution.py:242
  166.6 14.0 %collective-permute-start.20 = (bf16[512,512]{1,0:T(8,128)(2,1)}, bf16[512,512]{1,0:T(8,128)(2,1)S(1)}, u32[]{:S(2)}, u32[]{:S(2)}) collective-permute-start(bf16[512,512]{1,0:T(8,128)(2,1)} %serve.1.refs_0_), channel_id=1, source_target_pairs={{0,48},{16,0},{32,16},{48,32},{64,112},{80,64},{96,80},{112,96},{1... | collective-permute-start | bytes 1572872 | tf_op jit(solution)/shard_map/ppermute | solution.py:208
  167.8 13.8 %collective-permute-start.21 = (bf16[512,512]{1,0:T(8,128)(2,1)}, bf16[512,512]{1,0:T(8,128)(2,1)S(1)}, u32[]{:S(2)}, u32[]{:S(2)}) collective-permute-start(bf16[512,512]{1,0:T(8,128)(2,1)} %serve.1.refs_0_), channel_id=1, source_target_pairs={{0,16},{16,32},{32,48},{48,0},{64,80},{80,96},{96,112},{112,64},{1... | collective-permute-start | bytes 1572872 | tf_op jit(solution)/shard_map/ppermute | solution.py:208
  168.7 14.9 %collective-permute-start.22 = (bf16[512,512]{1,0:T(8,128)(2,1)}, bf16[512,512]{1,0:T(8,128)(2,1)S(1)}, u32[]{:S(2)}, u32[]{:S(2)}) collective-permute-start(bf16[512,512]{1,0:T(8,128)(2,1)} %serve.1.refs_0_), channel_id=1, source_target_pairs={{0,64},{16,80},{32,96},{48,112},{64,0},{80,16},{96,32},{112,48},{1... | collective-permute-start | bytes 1572872 | tf_op jit(solution)/shard_map/ppermute | solution.py:208
  184.4 11.7 %collective-permute-start.23 = (bf16[512,512]{1,0:T(8,128)(2,1)S(1)}, bf16[512,512]{1,0:T(8,128)(2,1)S(1)}, u32[]{:S(2)}, u32[]{:S(2)}) collective-permute-start(bf16[512,512]{1,0:T(8,128)(2,1)S(1)} %get-tuple-element.106), channel_id=1, source_target_pairs={{0,48},{16,0},{32,16},{48,32},{64,112},{80,64},{96,80},{112,96},{1... | collective-permute-start | bytes 1572872 | tf_op jit(solution)/shard_map/ppermute | solution.py:208
  186.2 10.4 %collective-permute-start.24 = (bf16[512,512]{1,0:T(8,128)(2,1)S(1)}, bf16[512,512]{1,0:T(8,128)(2,1)S(1)}, u32[]{:S(2)}, u32[]{:S(2)}) collective-permute-start(bf16[512,512]{1,0:T(8,128)(2,1)S(1)} %get-tuple-element.105), channel_id=1, source_target_pairs={{0,16},{16,32},{32,48},{48,0},{64,80},{80,96},{96,112},{112,64},{1... | collective-permute-start | bytes 1572872 | tf_op jit(solution)/shard_map/ppermute | solution.py:208
  186.4 13.4 %collective-permute-start.25 = (bf16[512,512]{1,0:T(8,128)(2,1)S(1)}, bf16[512,512]{1,0:T(8,128)(2,1)S(1)}, u32[]{:S(2)}, u32[]{:S(2)}) collective-permute-start(bf16[512,512]{1,0:T(8,128)(2,1)S(1)} %get-tuple-element.104), channel_id=1, source_target_pairs={{0,64},{16,80},{32,96},{48,112},{64,0},{80,16},{96,32},{112,48},{1... | collective-permute-start | bytes 1572872 | tf_op jit(solution)/shard_map/ppermute | solution.py:208
  196.1 12.4 %copy-start.5 = (bf16[512,512]{1,0:T(8,128)(2,1)}, bf16[512,512]{1,0:T(8,128)(2,1)S(1)}, u32[]{:S(2)}) copy-start(bf16[512,512]{1,0:T(8,128)(2,1)S(1)} %collective-permute-done.23.refs_0_) | copy-start | bytes 1572868
  196.6 11.9 %copy-start.6 = (bf16[512,512]{1,0:T(8,128)(2,1)}, bf16[512,512]{1,0:T(8,128)(2,1)S(1)}, u32[]{:S(2)}) copy-start(bf16[512,512]{1,0:T(8,128)(2,1)S(1)} %collective-permute-done.24.refs_1_) | copy-start | bytes 1572868
  199.8 8.7 %copy-start.10 = (bf16[512,512]{1,0:T(8,128)(2,1)}, bf16[512,512]{1,0:T(8,128)(2,1)S(1)}, u32[]{:S(2)}) copy-start(bf16[512,512]{1,0:T(8,128)(2,1)S(1)} %collective-permute-done.25.refs_2_) | copy-start | bytes 1572868
  199.8 13.4 %collective-permute-start.26 = (bf16[256,512]{1,0:T(8,128)(2,1)S(1)}, bf16[256,512]{1,0:T(8,128)(2,1)S(1)}, u32[]{:S(2)}, u32[]{:S(2)}) collective-permute-start(bf16[256,512]{1,0:T(8,128)(2,1)S(1)} %slice.182), channel_id=1, source_target_pairs={{0,48},{16,0},{32,16},{48,32},{64,112},{80,64},{96,80},{112,96},{1... | collective-permute-start | bytes 786440 | tf_op jit(solution)/shard_map/ppermute | solution.py:208
  200.3 13.0 %collective-permute-start.27 = (bf16[256,512]{1,0:T(8,128)(2,1)S(1)}, bf16[256,512]{1,0:T(8,128)(2,1)S(1)}, u32[]{:S(2)}, u32[]{:S(2)}) collective-permute-start(bf16[256,512]{1,0:T(8,128)(2,1)S(1)} %slice.183), channel_id=1, source_target_pairs={{0,64},{16,80},{32,96},{48,112},{64,0},{80,16},{96,32},{112,48},{1... | collective-permute-start | bytes 786440 | tf_op jit(solution)/shard_map/ppermute | solution.py:208
  (10 other events, 20.6 us)
where the time goes:
time: 217 us; the launch traced here: 216 us
  starting transfers between devices  75.3 us (35%)
  Pallas kernels  70 us (32%)
  waiting for transfers between devices  61.7 us (28%)
  other arithmetic  3.96 us (2%)
  local copies, waits for them, and re-layouts  3.82 us (2%)
    pallas_call x2, Pallas kernels, attend(): pl.pallas_call(functools.partial(attend_kernel, hp, ck, pieces, absolute)...  55 us
    ppermute x16, waiting for transfers between devices, fetch(): return lax.ppermute(value, 'dp', pairs)  37.2 us
    ppermute x16, starting transfers between devices, fetch(): return lax.ppermute(value, 'dp', pairs)  32.9 us
    all_to_all x3, starting transfers between devices, dp_sum(): got = lax.all_to_all(parts, 'dp', 0, 0, tiled=True)  21.5 us
    ppermute x12, waiting for transfers between devices, turn(): return lax.ppermute(value, 'replica', [(s, (s + by) % 4) for s in range(4)])  18.7 us
    ppermute x12, starting transfers between devices, turn(): return lax.ppermute(value, 'replica', [(s, (s + by) % 4) for s in range(4)])  16.3 us
    pallas_call x2, Pallas kernels, update(): pl.pallas_call(functools.partial(update_kernel, serve), out_shape=outs, i...  8.51 us
    pallas_call x3, Pallas kernels, place(): pl.pallas_call(functools.partial(place_kernel, pieces, len(started)), out...  6.47 us
  transfers between devices with their start and end apart: 32, of which 21 were waited for; matrix products, arithmetic and copies ran while one was open for 1% of the time, Pallas kernels for 30%

commit v1 on v0

--- a/solution.py
+++ b/solution.py
@@ -42,10 +42,10 @@
     return [lax.rem(here + j, 4) * size for j in range(4)]
 
 
-def attend_kernel(hp, ck, pieces, absolute, seg_ref, q_ref, do_ref, ko_ref, vo_ref, *refs):
+def attend_kernel(hp, ck, pieces, first, seg_ref, q_ref, do_ref, ko_ref, vo_ref, *refs):
     count = 1 + max(p[0] for p in pieces)
     arrays, refs = refs[:count], refs[count:]
-    sends, refs = refs[:5], refs[5:]
+    sends, refs = (refs[:1], refs[1:]) if first else (refs[:5], refs[5:])
     k_ref, v_ref, s_ref, p_ref, dp_ref, dk_acc, dv_acc, sems = refs
     keys = k_ref.shape[0]
     rows = hp * TOK
@@ -53,7 +53,7 @@
     chunks = keys // ck
     c = SCALE * LOG2E
 
-    starts = block_rows(keys // 8, absolute)
+    starts = block_rows(keys // 8, not first)
     loads = [[], []]
     for side, dst in enumerate((k_ref, v_ref)):
         for n, (array, src, size, block, low) in enumerate(pieces):
@@ -159,35 +159,35 @@
     state = lax.fori_loop(2, steps, lambda at, st: tick(at, True, True, True, st), state)
     state = tick(steps, False, True, True, state)
     tick(steps + 1, False, False, True, state)
-    send_keys, send_values = sends[0], sends[1:]
-    blocks, _, size, _ = send_keys.shape
+    blocks, _, size, _ = sends[0].shape
     turns = quarter_rows(size)
+    offsets = block_rows(4 * size, False)
     for j in range(4):
         for block in range(blocks):
             here = pl.ds(pl.multiple_of(block * 4 * size + turns[j], size), size)
-            send_keys[block, j] = (dk_acc[here, :] * SCALE).astype(BF16)
-            send_values[j][block] = dv_acc[here, :].astype(BF16)
-
-
-def attend(group, absolute, seg, queries, d_out, conv_keys, conv_values, arrays, pieces, hp=2, ck=2048):
+            sends[0][block, j, :, :HEAD] = (dk_acc[here, :] * SCALE).astype(BF16)
+            if first:
+                sends[0][block, j, :, HEAD:] = dv_acc[here, :].astype(BF16)
+            else:
+                there = pl.ds(pl.multiple_of(offsets[block] + turns[j], size), size)
+                sends[1 + j][2 * (block % 4) + block // 4] = dv_acc[there, :].astype(BF16)
+
+
+def attend(group, first, seg, queries, d_out, conv_keys, conv_values, arrays, pieces, hp=2, ck=2048):
     keys = sum(p[2] for p in pieces)
     rows = hp * TOK
-    anywhere = pl.BlockSpec(memory_space=pltpu.HBM)
+    anywhere = pl.BlockSpec(memory_space=pltpu.VMEM)
     wide = pl.BlockSpec((TOK, GROUP * HEAD), lambda i: (0, group))
     slim = pl.BlockSpec((TOK, HEAD), lambda i: (0, group))
+    size = keys // 32
+    sends = [(8, 4, size, 2 * HEAD)] if first else [(8, 4, size, HEAD)] + [(8, size, HEAD)] * 4
     return pl.pallas_call(
-        functools.partial(attend_kernel, hp, ck, pieces, absolute),
+        functools.partial(attend_kernel, hp, ck, pieces, first),
         grid=(1,),
-        out_shape=[
-            jax.ShapeDtypeStruct((8, 4, keys // 32, HEAD), BF16),
-            *[jax.ShapeDtypeStruct((8, keys // 32, HEAD), BF16)] * 4,
-        ],
+        out_shape=[jax.ShapeDtypeStruct(shape, BF16) for shape in sends],
         in_specs=[pl.BlockSpec((1, TOK), lambda i: (0, 0)), wide, wide, slim, slim]
         + [anywhere] * len(arrays),
-        out_specs=[
-            pl.BlockSpec((8, 4, keys // 32, HEAD), lambda i: (0, 0, 0, 0)),
-            *[pl.BlockSpec((8, keys // 32, HEAD), lambda i: (0, 0, 0))] * 4,
-        ],
+        out_specs=[pl.BlockSpec(shape, lambda i, n=len(shape): (0,) * n) for shape in sends],
         scratch_shapes=[pltpu.VMEM((keys, HEAD), BF16)] * 2
         + [pltpu.VMEM((keys, rows), F32)] * 3
         + [pltpu.VMEM((keys, HEAD), F32)] * 2
@@ -197,7 +197,7 @@
             bytes_accessed=8 << 20,
             transcendentals=GROUP * TOK * keys,
         ),
-        compiler_params=pltpu.CompilerParams(vmem_limit_bytes=56 << 20),
+        compiler_params=pltpu.CompilerParams(vmem_limit_bytes=50 << 20),
         name="attend",
     )(seg, queries, d_out, conv_keys, conv_values, *arrays)
 
@@ -238,6 +238,19 @@
     return whole + halves
 
 
+def deliver(value, offset):
+    z, y = offset
+    pairs = [(s, ((s // 4 + z) % 2) * 4 + (s % 4 + y) % 4) for s in range(8)]
+    return lax.ppermute(value, "dp", pairs)
+
+
+def lines_sum(parts):
+    sent = [deliver(parts[2 * i : 2 * i + 2], OFFSETS[i]) for i in (1, 2, 3)]
+    here, far = total([parts[:2], *sent])
+    far = deliver(far.astype(BF16), (1, 0))
+    return here + far.astype(F32)
+
+
 def turn(value, by):
     return lax.ppermute(value, "replica", [(s, (s + by) % 4) for s in range(4)])
 
@@ -272,27 +285,17 @@
 def place_kernel(pieces, skip, *refs):
     count = 1 + max(p[0] for p in pieces)
     arrays, refs = refs[:count], refs[count + skip :]
-    keys_ref, values_ref, hold, sems_in, sems_out = refs
+    keys_ref, values_ref, sems = refs
     half = keys_ref.shape[1]
     starts = block_rows(keys_ref.shape[0] // 8, False)
-    loads, at = [], 0
-    for n, (array, src, size, _, _) in enumerate(pieces):
-        load = pltpu.make_async_copy(
-            arrays[array].at[pl.ds(src, size), :], hold.at[pl.ds(at, size), :], sems_in.at[n]
-        )
-        load.start()
-        loads.append((load, at))
-        at += size
     stores = []
-    for n, (_, _, size, block, low) in enumerate(pieces):
-        load, at = loads[n]
-        load.wait()
+    for n, (array, src, size, block, low) in enumerate(pieces):
         to = pl.multiple_of(starts[block] + low, size)
         for side, out in enumerate((keys_ref, values_ref)):
             store = pltpu.make_async_copy(
-                hold.at[pl.ds(at, size), pl.ds(side * half, half)],
+                arrays[array].at[pl.ds(src, size), pl.ds(side * half, half)],
                 out.at[pl.ds(to, size), :],
-                sems_out.at[2 * n + side],
+                sems.at[2 * n + side],
             )
             store.start()
             stores.append(store)
@@ -301,42 +304,61 @@
 
 
 def place(arrays, pieces, keys, started=()):
-    rows, wide = sum(p[2] for p in pieces), arrays[0].shape[1]
+    wide = arrays[0].shape[1]
     out = jax.ShapeDtypeStruct((keys, wide // 2), BF16)
     anywhere = pl.BlockSpec(memory_space=pltpu.HBM)
     first = len(arrays)
     return pl.pallas_call(
         functools.partial(place_kernel, pieces, len(started)),
         out_shape=[out, out],
-        in_specs=[anywhere] * (len(arrays) + len(started)),
+        in_specs=[pl.BlockSpec(memory_space=pltpu.VMEM)] * first + [anywhere] * len(started),
         out_specs=[anywhere] * 2,
         input_output_aliases={first + i: i for i in range(len(started))},
-        scratch_shapes=[
-            pltpu.VMEM((rows, wide), BF16),
-            pltpu.SemaphoreType.DMA((len(pieces),)),
-            pltpu.SemaphoreType.DMA((2 * len(pieces),)),
-        ],
+        scratch_shapes=[pltpu.SemaphoreType.DMA((2 * len(pieces),))],
+        compiler_params=pltpu.CompilerParams(vmem_limit_bytes=16 << 20),
         name="place",
     )(*arrays, *started)
+
+
+def pack_kernel(keys_ref, values_ref, out_ref):
+    both = jnp.concatenate([keys_ref[...], values_ref[...]], axis=1).astype(BF16)
+    out_ref[...] = jnp.broadcast_to(both, out_ref.shape)
+
+
+def pack(head, keys, values, copies=()):
+    share = keys.shape[0]
+    shape = (*copies, share, 2 * HEAD)
+    half = pl.BlockSpec((share, HEAD), lambda i: (0, head))
+    return pl.pallas_call(
+        pack_kernel,
+        grid=(1,),
+        out_shape=jax.ShapeDtypeStruct(shape, BF16),
+        in_specs=[half, half],
+        out_specs=pl.BlockSpec(shape, lambda i: (0,) * len(shape)),
+        cost_estimate=pl.CostEstimate(flops=0, bytes_accessed=1 << 20, transcendentals=0),
+        name="pack",
+    )(keys, values)
 
 
 def update_kernel(serve, *refs):
     grads, olds, outs = refs[:4], refs[4:10], refs[10:]
     size = grads[0].shape[0]
-    half = grads[0].shape[1] // 2
     turns = quarter_rows(size)
     for j in range(4):
         at = pl.ds(pl.multiple_of(turns[j], size), size)
-        for side in range(2):
-            cols = slice(side * half, (side + 1) * half)
-            grad = grads[j][:, cols].astype(F32)
-            new = adamw_step(*[olds[2 * n + side][at, :] for n in range(3)], grad)
-            if serve:
-                outs[0][at, cols] = new[0].astype(BF16)
-            else:
-                for n in range(3):
-                    outs[2 * n + side][at, :] = new[n]
-                outs[6 + side][at, :] = grad
+        for head in range(2):
+            cols = slice(head * HEAD, (head + 1) * HEAD)
+            for side in range(2):
+                low = (2 * head + side) * HEAD
+                grad = grads[j][:, low : low + HEAD].astype(F32)
+                new = adamw_step(*[olds[2 * n + side][at, cols] for n in range(3)], grad)
+                if serve:
+                    low = (2 * side + head) * HEAD
+                    outs[0][at, low : low + HEAD] = new[0].astype(BF16)
+                else:
+                    for n in range(3):
+                        outs[2 * n + side][at, cols] = new[n]
+                    outs[6 + side][at, cols] = grad
 
 
 def update(serve, grads, olds):
@@ -351,6 +373,7 @@
         in_specs=[vm] * 10,
         out_specs=[vm] * len(outs),
         cost_estimate=pl.CostEstimate(flops=0, bytes_accessed=8 << 20, transcendentals=0),
+        compiler_params=pltpu.CompilerParams(vmem_limit_bytes=24 << 20),
         name="serve" if serve else "update",
     )(*grads, *olds)
 
@@ -371,30 +394,24 @@
     share = master_keys.shape[0]
     relayed = relay_pieces(share)
 
-    def own_block(head):
-        at = slice(head * HEAD, (head + 1) * HEAD)
-        return jnp.concatenate([master_keys[:, at], master_values[:, at]], axis=1).astype(BF16)
-
-    def attention(group, absolute, arrays, pieces):
+    def attention(group, arrays, pieces):
         tokens = (segment_ids, queries, d_out, conv_keys, conv_values)
-        return attend(group, absolute, *tokens, arrays, pieces)
-
-    later = jnp.broadcast_to(own_block(1), (8, share, 2 * HEAD))
-    first = relay_gather(own_block(0))
-    *first, later = lax.optimization_barrier((*first, later))
-    parts_first = attention(0, False, first, relayed)
+        return attend(group, group == 0, *tokens, arrays, pieces)
+
+    later = pack(1, master_keys, master_values, (8,))
+    first = relay_gather(pack(0, master_keys, master_values))
+    *early, later = lax.optimization_barrier((*first[:7], later))
+    first = (*early, *first[7:])
+    (both_part,) = attention(0, first, relayed)
     second = lax.all_to_all(later, "dp", 0, 0, tiled=True).reshape(8 * share, 2 * HEAD)
-    parts_second = attention(
-        1, True, [second], [(0, b * share, share, b, 0) for b in range(8)]
-    )
-    keys_sum = [dp_sum(parts[0]) for parts in (parts_first, parts_second)]
-    values_sum = [replica_sum(parts_first[1:])]
-    values_sum.append(replica_sum(parts_second[1:]))
-    keys_low = jnp.concatenate(keys_sum, axis=2).astype(BF16)
-    values_low = jnp.concatenate(values_sum, axis=2).astype(BF16)
-    keys_quarter = replica_sum([keys_low[j] for j in range(4)])
-    values_quarter = dp_sum(values_low)
-    both = jnp.concatenate([keys_quarter, values_quarter], axis=1).astype(BF16)
+    keys_part, *values_part = attention(1, [second], [(0, b * share, share, b, 0) for b in range(8)])
+    first_sum = dp_sum(both_part).astype(BF16)
+    keys_sum = dp_sum(keys_part)
+    values_sum = replica_sum(values_part).astype(BF16)
+    low = jnp.concatenate([first_sum, keys_sum.astype(BF16)], axis=2)
+    most = replica_sum([low[j] for j in range(4)])
+    rest = lines_sum(values_sum)
+    both = jnp.concatenate([most, rest], axis=1).astype(BF16)
     grads = [both] + [turn(both, -j) for j in (1, 2, 3)]
     olds = (master_keys, master_values, moment_keys, moment_values, second_keys, second_values)
     (served,) = update(True, grads, olds)

time: 217 us -> 227 us (1.046)
  waiting for transfers between devices: 61.7 us -> 82 us
  Pallas kernels: 70 us -> 65 us
  starting transfers between devices: 75.3 us -> 71.4 us
  local copies, waits for them, and re-layouts: 3.82 us -> 0.87 us
    ppermute x16, waiting for transfers between devices: 37.2 us -> 55.7 us  [fetch(): return lax.ppermute(value, 'dp', pairs)]
    all_to_all x3 -> x2, starting transfers between devices: 21.5 us -> 11.8 us  [dp_sum(): got = lax.all_to_all(parts, 'dp', 0, 0, tiled=True)]
    ppermute x0 -> x4, starting transfers between devices: none -> 8.59 us  [deliver(): return lax.ppermute(value, 'dp', pairs)]
    ppermute x0 -> x4, waiting for transfers between devices: none -> 8.23 us  [deliver(): return lax.ppermute(value, 'dp', pairs)]
    all_to_all x3 -> x2, waiting for transfers between devices: 5.74 us -> 0.01 us  [dp_sum(): got = lax.all_to_all(parts, 'dp', 0, 0, tiled=True)]
    pallas_call x2, Pallas kernels: 8.51 us -> 3.6 us  [update(): pl.pallas_call(functools.partial(update_kernel, serve), out_shape=outs, i...]
    add x3, other arithmetic: 0.36 us -> 4.07 us  [total(): parts = [a + b for a, b in zip(parts[::2], parts[1::2])]]
    pallas_call x3, Pallas kernels: 6.47 us -> 3.45 us  [place(): pl.pallas_call(functools.partial(place_kernel, pieces, len(started)), out...]
  transfers between devices with their start and end apart: 32 -> 32, of which waited for: 21 -> 24; matrix products, arithmetic and copies ran while one was open for 1% -> 3% of each run, Pallas kernels for 30% -> 27%
where the time goes in v1:
time: 227 us
  waiting for transfers between devices  82 us (36%)
  starting transfers between devices  71.4 us (31%)
  Pallas kernels  65 us (29%)
  other arithmetic  6.05 us (3%)
    ppermute x16, waiting for transfers between devices, fetch(): return lax.ppermute(value, 'dp', pairs)  55.7 us
    pallas_call x2, Pallas kernels, attend(): pl.pallas_call(functools.partial(attend_kernel, hp, ck, pieces, first), g...  53.7 us
    ppermute x16, starting transfers between devices, fetch(): return lax.ppermute(value, 'dp', pairs)  30.2 us
    ppermute x9, waiting for transfers between devices, turn(): return lax.ppermute(value, 'replica', [(s, (s + by) % 4) for s in range(4)])  18.1 us
    ppermute x9, starting transfers between devices, turn(): return lax.ppermute(value, 'replica', [(s, (s + by) % 4) for s in range(4)])  13.8 us
    all_to_all x2, starting transfers between devices, dp_sum(): got = lax.all_to_all(parts, 'dp', 0, 0, tiled=True)  11.8 us
    ppermute x4, starting transfers between devices, deliver(): return lax.ppermute(value, 'dp', pairs)  8.59 us
    ppermute x4, waiting for transfers between devices, deliver(): return lax.ppermute(value, 'dp', pairs)  8.23 us
  transfers between devices with their start and end apart: 32, of which 24 were waited for; matrix products, arithmetic and copies ran while one was open for 3% of the time, Pallas kernels for 27%

profile of v1, /device:TPU:0, one launch (start us, length us, event | category | flops | bytes accessed | tf_op | source)
XLA Modules:
  0.0 226.5 jit_solution(14460881649750330611)
XLA Ops:
  0.6 1.8 pack.2.refs_0_
  2.4 3.1 %collective-permute-start = (bf16[512,256]{1,0:T(8,128)(2,1)}, bf16[512,256]{1,0:T(8,128)(2,1)S(1)}, u32[]{:S(2)}, u32[]{:S(2)}) collective-permute-start(bf16[512,256]{1,0:T(8,128)(2,1)} %pack.2.refs_0_), channel_id=1, source_target_pairs={{0,48},{16,0},{32,16},{48,32},{64,112},{80,64},{96,80},{112,96},{1... | collective-permute-start | bytes 786440 | tf_op jit(solution)/shard_map/ppermute | solution.py:208
  5.5 3.9 %collective-permute-start.2 = (bf16[512,256]{1,0:T(8,128)(2,1)}, bf16[512,256]{1,0:T(8,128)(2,1)S(1)}, u32[]{:S(2)}, u32[]{:S(2)}) collective-permute-start(bf16[512,256]{1,0:T(8,128)(2,1)} %pack.2.refs_0_), channel_id=1, source_target_pairs={{0,64},{16,80},{32,96},{48,112},{64,0},{80,16},{96,32},{112,48},{1... | collective-permute-start | bytes 786440 | tf_op jit(solution)/shard_map/ppermute | solution.py:208
  9.4 2.0 collective-permute-done.refs_1_
  11.4 3.3 %collective-permute-done.1.refs_2_ = bf16[512,256]{1,0:T(8,128)(2,1)S(1)} collective-permute-done((bf16[512,256]{1,0:T(8,128)(2,1)}, bf16[512,256]{1,0:T(8,128)(2,1)S(1)}, u32[]{:S(2)}, u32[]{:S(2)}) %collective-permute-start.1) | collective-permute-done | bytes 262176 | tf_op jit(solution)/shard_map/ppermute | solution.py:208
  16.6 2.9 %collective-permute-start.3 = (bf16[512,256]{1,0:T(8,128)(2,1)}, bf16[512,256]{1,0:T(8,128)(2,1)S(1)}, u32[]{:S(2)}, u32[]{:S(2)}) collective-permute-start(bf16[512,256]{1,0:T(8,128)(2,1)} %get-tuple-element.103), channel_id=1, source_target_pairs={{0,48},{16,0},{32,16},{48,32},{64,112},{80,64},{96,80},{112,96},{1... | collective-permute-start | bytes 786440 | tf_op jit(solution)/shard_map/ppermute | solution.py:208
  19.5 3.2 %collective-permute-start.5 = (bf16[512,256]{1,0:T(8,128)(2,1)S(1)}, bf16[512,256]{1,0:T(8,128)(2,1)S(1)}, u32[]{:S(2)}, u32[]{:S(2)}) collective-permute-start(bf16[512,256]{1,0:T(8,128)(2,1)S(1)} %get-tuple-element.101), channel_id=1, source_target_pairs={{0,64},{16,80},{32,96},{48,112},{64,0},{80,16},{96,32},{112,48},{1... | collective-permute-start | bytes 786440 | tf_op jit(solution)/shard_map/ppermute | solution.py:208
  22.7 2.5 %pack.3 = bf16[8,512,256]{2,1,0:T(8,128)(2,1)} custom-call(f32[512,256]{1,0:T(8,128)} %refs_4_.3, f32[512,256]{1,0:T(8,128)} %refs_5_.3), custom_call_target="tpu_custom_call" | custom-call | bytes 1048576 | tf_op jit(solution)/shard_map/pack/pallas_call | solution.py:332
  25.3 2.3 %collective-permute-done.4.refs_5_ = bf16[512,256]{1,0:T(8,128)(2,1)S(1)} collective-permute-done((bf16[512,256]{1,0:T(8,128)(2,1)}, bf16[512,256]{1,0:T(8,128)(2,1)S(1)}, u32[]{:S(2)}, u32[]{:S(2)}) %collective-permute-start.4) | collective-permute-done | bytes 262176 | tf_op jit(solution)/shard_map/ppermute | solution.py:208
  27.7 6.9 %all-to-all-start.1 = ((bf16[8,512,256]{2,1,0:T(8,128)(2,1)}), bf16[8,512,256]{2,1,0:T(8,128)(2,1)}, u32[]{:S(2)}, u32[]{:S(2)}) async-start(bf16[8,512,256]{2,1,0:T(8,128)(2,1)} %pack.3), calls=%async_computation.1 | async-start | bytes 4194304 | tf_op jit(solution)/shard_map/all_to_all | solution.py:406
  34.6 3.3 %collective-permute-start.6 = (bf16[256,256]{1,0:T(8,128)(2,1)S(1)}, bf16[256,256]{1,0:T(8,128)(2,1)S(1)}, u32[]{:S(2)}, u32[]{:S(2)}) collective-permute-start(bf16[256,256]{1,0:T(8,128)(2,1)S(1)} %slice.116), channel_id=1, source_target_pairs={{0,48},{16,0},{32,16},{48,32},{64,112},{80,64},{96,80},{112,96},{1... | collective-permute-start | bytes 393224 | tf_op jit(solution)/shard_map/ppermute | solution.py:208
  37.9 3.0 %collective-permute-start.7 = (bf16[256,256]{1,0:T(8,128)(2,1)S(1)}, bf16[256,256]{1,0:T(8,128)(2,1)S(1)}, u32[]{:S(2)}, u32[]{:S(2)}) collective-permute-start(bf16[256,256]{1,0:T(8,128)(2,1)S(1)} %slice.117), channel_id=1, source_target_pairs={{0,64},{16,80},{32,96},{48,112},{64,0},{80,16},{96,32},{112,48},{1... | collective-permute-start | bytes 393224 | tf_op jit(solution)/shard_map/ppermute | solution.py:208
  40.9 18.6 %collective-permute-done.6.refs_7_ = bf16[256,256]{1,0:T(8,128)(2,1)S(1)} collective-permute-done((bf16[256,256]{1,0:T(8,128)(2,1)S(1)}, bf16[256,256]{1,0:T(8,128)(2,1)S(1)}, u32[]{:S(2)}, u32[]{:S(2)}) %collective-permute-start.6) | collective-permute-done | bytes 131104 | tf_op jit(solution)/shard_map/ppermute | solution.py:208
  59.5 1.4 collective-permute-done.7.refs_8_
  60.9 26.8 %attend.2 = bf16[8,4,128,256]{3,2,1,0:T(8,128)(2,1)} custom-call(s32[1,256]{1,0:T(1,128)S(1)} %copy-done.10, bf16[256,2048]{1,0:T(8,128)(2,1)S(1)} %copy-done.7, bf16[256,2048]{1,0:T(8,128)(2,1)} %do_ref.3, bf16[256,256]{1,0:T(8,128)(2,1)S(1)} %copy-done.8, bf16[256,256]{1,0:T(8,128)(2,1)S(1)} %copy-done.9, bf16[512,256]{1,0:T(8,128)(2,1)S(1)} %copy-done.6, ...), custom_call_target="tpu_custom_call" | custom-call | flops 8589934592 | bytes 8388608 | tf_op jit(solution)/shard_map/attend/pallas_call | solution.py:184
  87.7 4.9 %all-to-all-start = ((bf16[8,4,128,256]{3,2,1,0:T(8,128)(2,1)}), bf16[8,4,128,256]{3,2,1,0:T(8,128)(2,1)}, u32[]{:S(2)}, u32[]{:S(2)}) async-start(bf16[8,4,128,256]{3,2,1,0:T(8,128)(2,1)} %attend.2), calls=%async_computation | async-start | bytes 4194304 | tf_op jit(solution)/shard_map/all_to_all | solution.py:266
  92.6 26.9 %attend.3 = (bf16[8,4,128,128]{3,2,1,0:T(8,128)(2,1)}, bf16[8,128,128]{2,1,0:T(8,128)(2,1)S(1)}, bf16[8,128,128]{2,1,0:T(8,128)(2,1)S(1)}, bf16[8,128,128]{2,1,0:T(8,128)(2,1)S(1)}, bf16[8,128,128]{2,1,0:T(8,128)(2,1)S(1)}) custom-call(s32[1,256]{1,0:T(1,128)S(1)} %copy-done.10, bf16[256,2048]{1,0:T(8,128)(2,1)S(1)} %copy-done.7, bf16[256,2048]{1,0:T(8,128)(2,1)} %do_ref.3, ...), custom_call_target="tpu_custom_call" | custom-call | flops 8589934592 | bytes 8388608 | tf_op jit(solution)/shard_map/attend/pallas_call | solution.py:184
  119.6 1.5 collective-permute-start.11
  121.1 1.8 collective-permute-start.12
  122.9 1.8 collective-permute-start.13
  124.7 4.3 %collective-permute-done.11 = bf16[8,128,128]{2,1,0:T(8,128)(2,1)S(1)} collective-permute-done((bf16[8,128,128]{2,1,0:T(8,128)(2,1)S(1)}, bf16[8,128,128]{2,1,0:T(8,128)(2,1)S(1)}, u32[]{:S(2)}, u32[]{:S(2)}) %collective-permute-start.11) | collective-permute-done | bytes 262176 | tf_op jit(solution)/shard_map/ppermute | solution.py:255
  129.0 3.7 %collective-permute-done.12 = bf16[8,128,128]{2,1,0:T(8,128)(2,1)S(1)} collective-permute-done((bf16[8,128,128]{2,1,0:T(8,128)(2,1)S(1)}, bf16[8,128,128]{2,1,0:T(8,128)(2,1)S(1)}, u32[]{:S(2)}, u32[]{:S(2)}) %collective-permute-start.12) | collective-permute-done | bytes 262176 | tf_op jit(solution)/shard_map/ppermute | solution.py:255
  132.7 1.7 collective-permute-done.13
  134.6 6.9 %all-to-all-start.2 = ((bf16[8,4,128,128]{3,2,1,0:T(8,128)(2,1)}), bf16[8,4,128,128]{3,2,1,0:T(8,128)(2,1)}, u32[]{:S(2)}, u32[]{:S(2)}) async-start(bf16[8,4,128,128]{3,2,1,0:T(8,128)(2,1)} %get-tuple-element.63), calls=%async_computation.2 | async-start | bytes 2097152 | tf_op jit(solution)/shard_map/all_to_all | solution.py:266
  141.6 2.1 collective-permute-start.14
  143.6 1.6 collective-permute-start.15
  145.2 2.0 collective-permute-start.16
  147.2 1.8 fusion
  149.0 7.2 %collective-permute-done.14 = bf16[2,128,128]{2,1,0:T(8,128)(2,1)S(1)} collective-permute-done((bf16[2,128,128]{2,1,0:T(8,128)(2,1)S(1)}, bf16[2,128,128]{2,1,0:T(8,128)(2,1)S(1)}, u32[]{:S(2)}, u32[]{:S(2)}) %collective-permute-start.14) | collective-permute-done | bytes 65568 | tf_op jit(solution)/shard_map/ppermute | solution.py:244
  158.8 3.0 %collective-permute-start.17 = (bf16[128,128]{1,0:T(8,128)(2,1)}, bf16[128,128]{1,0:T(8,128)(2,1)}, u32[]{:S(2)}, u32[]{:S(2)}) collective-permute-start(bf16[128,128]{1,0:T(8,128)(2,1)} %fusion.13), channel_id=1, source_target_pairs={{0,64},{16,80},{32,96},{48,112},{64,0},{80,16},{96,32},{112,48},{1... | collective-permute-start | bytes 98312 | tf_op jit(solution)/shard_map/ppermute | solution.py:244
  161.7 1.4 fusion.3
  164.0 1.3 collective-permute-start.8
  165.3 2.0 collective-permute-start.9
  168.0 1.4 collective-permute-done.10
  170.5 2.7 %collective-permute-start.18 = (bf16[128,512]{1,0:T(8,128)(2,1)S(1)}, bf16[128,512]{1,0:T(8,128)(2,1)S(1)}, u32[]{:S(2)}, u32[]{:S(2)}) collective-permute-start(bf16[128,512]{1,0:T(8,128)(2,1)S(1)} %pad_maximum_fusion.6.refs_0_), channel_id=1, source_target_pairs={{0,3},{1,0},{2,1},{3,2},{4,7},{5,4},{6,5},{7,6},{8,11},{9,8},{10,9... | collective-permute-start | bytes 393224 | tf_op jit(solution)/shard_map/ppermute | solution.py:255
  175.8 4.0 %collective-permute-done.19.refs_2_ = bf16[128,512]{1,0:T(8,128)(2,1)S(1)} collective-permute-done((bf16[128,512]{1,0:T(8,128)(2,1)S(1)}, bf16[128,512]{1,0:T(8,128)(2,1)S(1)}, u32[]{:S(2)}, u32[]{:S(2)}) %collective-permute-start.19) | collective-permute-done | bytes 131104 | tf_op jit(solution)/shard_map/ppermute | solution.py:255
  179.8 1.3 collective-permute-done.20.refs_3_
  182.0 3.3 %collective-permute-start.21 = (bf16[512,512]{1,0:T(8,128)(2,1)S(1)}, bf16[512,512]{1,0:T(8,128)(2,1)S(1)}, u32[]{:S(2)}, u32[]{:S(2)}) collective-permute-start(bf16[512,512]{1,0:T(8,128)(2,1)S(1)} %serve.1.refs_0_), channel_id=1, source_target_pairs={{0,48},{16,0},{32,16},{48,32},{64,112},{80,64},{96,80},{112,96},{1... | collective-permute-start | bytes 1572872 | tf_op jit(solution)/shard_map/ppermute | solution.py:208
  185.9 8.2 %collective-permute-done.21.refs_1_ = bf16[512,512]{1,0:T(8,128)(2,1)S(1)} collective-permute-done((bf16[512,512]{1,0:T(8,128)(2,1)S(1)}, bf16[512,512]{1,0:T(8,128)(2,1)S(1)}, u32[]{:S(2)}, u32[]{:S(2)}) %collective-permute-start.21) | collective-permute-done | bytes 524320 | tf_op jit(solution)/shard_map/ppermute | solution.py:208
  194.1 4.0 %collective-permute-done.22.refs_2_ = bf16[512,512]{1,0:T(8,128)(2,1)S(1)} collective-permute-done((bf16[512,512]{1,0:T(8,128)(2,1)S(1)}, bf16[512,512]{1,0:T(8,128)(2,1)S(1)}, u32[]{:S(2)}, u32[]{:S(2)}) %collective-permute-start.22) | collective-permute-done | bytes 524320 | tf_op jit(solution)/shard_map/ppermute | solution.py:208
  198.4 3.8 %collective-permute-start.24 = (bf16[512,512]{1,0:T(8,128)(2,1)S(1)}, bf16[512,512]{1,0:T(8,128)(2,1)S(1)}, u32[]{:S(2)}, u32[]{:S(2)}) collective-permute-start(bf16[512,512]{1,0:T(8,128)(2,1)S(1)} %get-tuple-element.95), channel_id=1, source_target_pairs={{0,48},{16,0},{32,16},{48,32},{64,112},{80,64},{96,80},{112,96},{1... | collective-permute-start | bytes 1572872 | tf_op jit(solution)/shard_map/ppermute | solution.py:208
  202.8 8.9 %collective-permute-done.24.refs_0_ = bf16[512,512]{1,0:T(8,128)(2,1)S(1)} collective-permute-done((bf16[512,512]{1,0:T(8,128)(2,1)S(1)}, bf16[512,512]{1,0:T(8,128)(2,1)S(1)}, u32[]{:S(2)}, u32[]{:S(2)}) %collective-permute-start.24) | collective-permute-done | bytes 524320 | tf_op jit(solution)/shard_map/ppermute | solution.py:208
  212.6 3.1 %collective-permute-done.26.refs_2_ = bf16[512,512]{1,0:T(8,128)(2,1)S(1)} collective-permute-done((bf16[512,512]{1,0:T(8,128)(2,1)S(1)}, bf16[512,512]{1,0:T(8,128)(2,1)S(1)}, u32[]{:S(2)}, u32[]{:S(2)}) %collective-permute-start.26) | collective-permute-done | bytes 524320 | tf_op jit(solution)/shard_map/ppermute | solution.py:208
  215.7 1.9 collective-permute-start.27
  218.2 2.7 %update.1 = (f32[512,256]{1,0:T(8,128)}, f32[512,256]{1,0:T(8,128)}, f32[512,256]{1,0:T(8,128)}, f32[512,256]{1,0:T(8,128)}, f32[512,256]{1,0:T(8,128)}, /*index...) custom-call(bf16[128,512]{1,0:T(8,128)(2,1)S(1)} %pad_maximum_fusion.6.refs_0_, ...), custom_call_target="tpu_custom_call" | custom-call | bytes 8388608 | tf_op jit(solution)/shard_map/update/pallas_call | solution.py:370
  221.0 1.4 place.3
  222.3 1.3 place.4
  223.6 1.9 collective-permute-done.28.refs_1_
  (71 shorter events, 14.8 us)
Async XLA Ops:
  2.4 9.0 %collective-permute-start = (bf16[512,256]{1,0:T(8,128)(2,1)}, bf16[512,256]{1,0:T(8,128)(2,1)S(1)}, u32[]{:S(2)}, u32[]{:S(2)}) collective-permute-start(bf16[512,256]{1,0:T(8,128)(2,1)} %pack.2.refs_0_), channel_id=1, source_target_pairs={{0,48},{16,0},{32,16},{48,32},{64,112},{80,64},{96,80},{112,96},{1... | collective-permute-start | bytes 786440 | tf_op jit(solution)/shard_map/ppermute | solution.py:208
  5.5 9.2 %collective-permute-start.1 = (bf16[512,256]{1,0:T(8,128)(2,1)}, bf16[512,256]{1,0:T(8,128)(2,1)S(1)}, u32[]{:S(2)}, u32[]{:S(2)}) collective-permute-start(bf16[512,256]{1,0:T(8,128)(2,1)} %pack.2.refs_0_), channel_id=1, source_target_pairs={{0,16},{16,32},{32,48},{48,0},{64,80},{80,96},{96,112},{112,64},{1... | collective-permute-start | bytes 786440 | tf_op jit(solution)/shard_map/ppermute | solution.py:208
  5.5 10.2 %collective-permute-start.2 = (bf16[512,256]{1,0:T(8,128)(2,1)}, bf16[512,256]{1,0:T(8,128)(2,1)S(1)}, u32[]{:S(2)}, u32[]{:S(2)}) collective-permute-start(bf16[512,256]{1,0:T(8,128)(2,1)} %pack.2.refs_0_), channel_id=1, source_target_pairs={{0,64},{16,80},{32,96},{48,112},{64,0},{80,16},{96,32},{112,48},{1... | collective-permute-start | bytes 786440 | tf_op jit(solution)/shard_map/ppermute | solution.py:208
  16.6 8.7 %collective-permute-start.3 = (bf16[512,256]{1,0:T(8,128)(2,1)}, bf16[512,256]{1,0:T(8,128)(2,1)S(1)}, u32[]{:S(2)}, u32[]{:S(2)}) collective-permute-start(bf16[512,256]{1,0:T(8,128)(2,1)} %get-tuple-element.103), channel_id=1, source_target_pairs={{0,48},{16,0},{32,16},{48,32},{64,112},{80,64},{96,80},{112,96},{1... | collective-permute-start | bytes 786440 | tf_op jit(solution)/shard_map/ppermute | solution.py:208
  19.5 8.1 %collective-permute-start.4 = (bf16[512,256]{1,0:T(8,128)(2,1)}, bf16[512,256]{1,0:T(8,128)(2,1)S(1)}, u32[]{:S(2)}, u32[]{:S(2)}) collective-permute-start(bf16[512,256]{1,0:T(8,128)(2,1)} %get-tuple-element.102), channel_id=1, source_target_pairs={{0,16},{16,32},{32,48},{48,0},{64,80},{80,96},{96,112},{112,64},{1... | collective-permute-start | bytes 786440 | tf_op jit(solution)/shard_map/ppermute | solution.py:208
  19.5 8.1 %collective-permute-start.5 = (bf16[512,256]{1,0:T(8,128)(2,1)S(1)}, bf16[512,256]{1,0:T(8,128)(2,1)S(1)}, u32[]{:S(2)}, u32[]{:S(2)}) collective-permute-start(bf16[512,256]{1,0:T(8,128)(2,1)S(1)} %get-tuple-element.101), channel_id=1, source_target_pairs={{0,64},{16,80},{32,96},{48,112},{64,0},{80,16},{96,32},{112,48},{1... | collective-permute-start | bytes 786440 | tf_op jit(solution)/shard_map/ppermute | solution.py:208
  25.2 35.6 %copy-start.6 = (bf16[512,256]{1,0:T(8,128)(2,1)S(1)}, bf16[512,256]{1,0:T(8,128)(2,1)}, u32[]{:S(2)}) copy-start(bf16[512,256]{1,0:T(8,128)(2,1)} %pack.2.refs_0_) | copy-start | bytes 786436
  25.2 35.6 %copy-start.7 = (bf16[256,2048]{1,0:T(8,128)(2,1)S(1)}, bf16[256,2048]{1,0:T(8,128)(2,1)}, u32[]{:S(2)}) copy-start(bf16[256,2048]{1,0:T(8,128)(2,1)} %q_ref.3) | copy-start | bytes 3145732
  25.2 35.6 %copy-start.8 = (bf16[256,256]{1,0:T(8,128)(2,1)S(1)}, bf16[256,256]{1,0:T(8,128)(2,1)}, u32[]{:S(2)}) copy-start(bf16[256,256]{1,0:T(8,128)(2,1)} %ko_ref.3) | copy-start | bytes 393220
  25.2 35.7 %copy-start.9 = (bf16[256,256]{1,0:T(8,128)(2,1)S(1)}, bf16[256,256]{1,0:T(8,128)(2,1)}, u32[]{:S(2)}) copy-start(bf16[256,256]{1,0:T(8,128)(2,1)} %vo_ref.3) | copy-start | bytes 393220
  25.2 35.7 %copy-start.10 = (s32[1,256]{1,0:T(1,128)S(1)}, s32[1,256]{1,0:T(1,128)}, u32[]{:S(2)}) copy-start(s32[1,256]{1,0:T(1,128)} %seg_ref.3) | copy-start | bytes 3076
  27.7 60.1 %all-to-all-start.1 = ((bf16[8,512,256]{2,1,0:T(8,128)(2,1)}), bf16[8,512,256]{2,1,0:T(8,128)(2,1)}, u32[]{:S(2)}, u32[]{:S(2)}) async-start(bf16[8,512,256]{2,1,0:T(8,128)(2,1)} %pack.3), calls=%async_computation.1 | async-start | bytes 4194304 | tf_op jit(solution)/shard_map/all_to_all | solution.py:406
  34.6 24.9 %collective-permute-start.6 = (bf16[256,256]{1,0:T(8,128)(2,1)S(1)}, bf16[256,256]{1,0:T(8,128)(2,1)S(1)}, u32[]{:S(2)}, u32[]{:S(2)}) collective-permute-start(bf16[256,256]{1,0:T(8,128)(2,1)S(1)} %slice.116), channel_id=1, source_target_pairs={{0,48},{16,0},{32,16},{48,32},{64,112},{80,64},{96,80},{112,96},{1... | collective-permute-start | bytes 393224 | tf_op jit(solution)/shard_map/ppermute | solution.py:208
  37.9 23.0 %collective-permute-start.7 = (bf16[256,256]{1,0:T(8,128)(2,1)S(1)}, bf16[256,256]{1,0:T(8,128)(2,1)S(1)}, u32[]{:S(2)}, u32[]{:S(2)}) collective-permute-start(bf16[256,256]{1,0:T(8,128)(2,1)S(1)} %slice.117), channel_id=1, source_target_pairs={{0,64},{16,80},{32,96},{48,112},{64,0},{80,16},{96,32},{112,48},{1... | collective-permute-start | bytes 393224 | tf_op jit(solution)/shard_map/ppermute | solution.py:208
  87.7 46.9 %all-to-all-start = ((bf16[8,4,128,256]{3,2,1,0:T(8,128)(2,1)}), bf16[8,4,128,256]{3,2,1,0:T(8,128)(2,1)}, u32[]{:S(2)}, u32[]{:S(2)}) async-start(bf16[8,4,128,256]{3,2,1,0:T(8,128)(2,1)} %attend.2), calls=%async_computation | async-start | bytes 4194304 | tf_op jit(solution)/shard_map/all_to_all | solution.py:266
  119.6 9.4 %collective-permute-start.11 = (bf16[8,128,128]{2,1,0:T(8,128)(2,1)S(1)}, bf16[8,128,128]{2,1,0:T(8,128)(2,1)S(1)}, u32[]{:S(2)}, u32[]{:S(2)}) collective-permute-start(bf16[8,128,128]{2,1,0:T(8,128)(2,1)S(1)} %get-tuple-element.65), channel_id=1, source_target_pairs={{0,1},{1,2},{2,3},{3,0},{4,5},{5,6},{6,7},{7,4},{8,9},{9,10},{10,1... | collective-permute-start | bytes 786440 | tf_op jit(solution)/shard_map/ppermute | solution.py:255
  121.1 11.6 %collective-permute-start.12 = (bf16[8,128,128]{2,1,0:T(8,128)(2,1)S(1)}, bf16[8,128,128]{2,1,0:T(8,128)(2,1)S(1)}, u32[]{:S(2)}, u32[]{:S(2)}) collective-permute-start(bf16[8,128,128]{2,1,0:T(8,128)(2,1)S(1)} %get-tuple-element.66), channel_id=1, source_target_pairs={{0,3},{1,0},{2,1},{3,2},{4,7},{5,4},{6,5},{7,6},{8,11},{9,8},{10,9... | collective-permute-start | bytes 786440 | tf_op jit(solution)/shard_map/ppermute | solution.py:255
  122.9 11.6 %collective-permute-start.13 = (bf16[8,128,128]{2,1,0:T(8,128)(2,1)S(1)}, bf16[8,128,128]{2,1,0:T(8,128)(2,1)S(1)}, u32[]{:S(2)}, u32[]{:S(2)}) collective-permute-start(bf16[8,128,128]{2,1,0:T(8,128)(2,1)S(1)} %get-tuple-element.67), channel_id=1, source_target_pairs={{0,2},{1,3},{2,0},{3,1},{4,6},{5,7},{6,4},{7,5},{8,10},{9,11},{10,... | collective-permute-start | bytes 786440 | tf_op jit(solution)/shard_map/ppermute | solution.py:255
  134.6 12.6 %copy-start.11 = (bf16[8,128,128]{2,1,0:T(8,128)(2,1)}, bf16[8,128,128]{2,1,0:T(8,128)(2,1)S(1)}, u32[]{:S(2)}) copy-start(bf16[8,128,128]{2,1,0:T(8,128)(2,1)S(1)} %add_convert_fusion) | copy-start | bytes 786436
  134.6 27.1 %all-to-all-start.2 = ((bf16[8,4,128,128]{3,2,1,0:T(8,128)(2,1)}), bf16[8,4,128,128]{3,2,1,0:T(8,128)(2,1)}, u32[]{:S(2)}, u32[]{:S(2)}) async-start(bf16[8,4,128,128]{3,2,1,0:T(8,128)(2,1)} %get-tuple-element.63), calls=%async_computation.2 | async-start | bytes 2097152 | tf_op jit(solution)/shard_map/all_to_all | solution.py:266
  141.6 14.7 %collective-permute-start.14 = (bf16[2,128,128]{2,1,0:T(8,128)(2,1)S(1)}, bf16[2,128,128]{2,1,0:T(8,128)(2,1)S(1)}, u32[]{:S(2)}, u32[]{:S(2)}) collective-permute-start(bf16[2,128,128]{2,1,0:T(8,128)(2,1)S(1)} %get-tuple-element.96), channel_id=1, source_target_pairs={{0,16},{16,32},{32,48},{48,0},{64,80},{80,96},{96,112},{112,64},{1... | collective-permute-start | bytes 196616 | tf_op jit(solution)/shard_map/ppermute | solution.py:244
  143.6 12.6 %collective-permute-start.15 = (bf16[2,128,128]{2,1,0:T(8,128)(2,1)S(1)}, bf16[2,128,128]{2,1,0:T(8,128)(2,1)S(1)}, u32[]{:S(2)}, u32[]{:S(2)}) collective-permute-start(bf16[2,128,128]{2,1,0:T(8,128)(2,1)S(1)} %get-tuple-element.98), channel_id=1, source_target_pairs={{0,48},{16,0},{32,16},{48,32},{64,112},{80,64},{96,80},{112,96},{1... | collective-permute-start | bytes 196616 | tf_op jit(solution)/shard_map/ppermute | solution.py:244
  145.2 12.1 %collective-permute-start.16 = (bf16[2,128,128]{2,1,0:T(8,128)(2,1)S(1)}, bf16[2,128,128]{2,1,0:T(8,128)(2,1)S(1)}, u32[]{:S(2)}, u32[]{:S(2)}) collective-permute-start(bf16[2,128,128]{2,1,0:T(8,128)(2,1)S(1)} %get-tuple-element.97), channel_id=1, source_target_pairs={{0,32},{16,48},{32,0},{48,16},{64,96},{80,112},{96,64},{112,80},{1... | collective-permute-start | bytes 196616 | tf_op jit(solution)/shard_map/ppermute | solution.py:244
  149.0 32.2 %copy-start = (f32[512,256]{1,0:T(8,128)S(1)}, f32[512,256]{1,0:T(8,128)}, u32[]{:S(2)}) copy-start(f32[512,256]{1,0:T(8,128)} %refs_4_.3) | copy-start | bytes 1572868
  149.0 32.1 %copy-start.1 = (f32[512,256]{1,0:T(8,128)S(1)}, f32[512,256]{1,0:T(8,128)}, u32[]{:S(2)}) copy-start(f32[512,256]{1,0:T(8,128)} %refs_5_.3) | copy-start | bytes 1572868
  149.0 32.1 %copy-start.2 = (f32[512,256]{1,0:T(8,128)S(1)}, f32[512,256]{1,0:T(8,128)}, u32[]{:S(2)}) copy-start(f32[512,256]{1,0:T(8,128)} %refs_6_.3) | copy-start | bytes 1572868
  149.0 32.1 %copy-start.3 = (f32[512,256]{1,0:T(8,128)S(1)}, f32[512,256]{1,0:T(8,128)}, u32[]{:S(2)}) copy-start(f32[512,256]{1,0:T(8,128)} %refs_7_.3) | copy-start | bytes 1572868
  149.0 32.1 %copy-start.4 = (f32[512,256]{1,0:T(8,128)S(1)}, f32[512,256]{1,0:T(8,128)}, u32[]{:S(2)}) copy-start(f32[512,256]{1,0:T(8,128)} %refs_8_.3) | copy-start | bytes 1572868
  149.0 32.1 %copy-start.5 = (f32[512,256]{1,0:T(8,128)S(1)}, f32[512,256]{1,0:T(8,128)}, u32[]{:S(2)}) copy-start(f32[512,256]{1,0:T(8,128)} %refs_9_.3) | copy-start | bytes 1572868
  158.8 8.5 %collective-permute-start.17 = (bf16[128,128]{1,0:T(8,128)(2,1)}, bf16[128,128]{1,0:T(8,128)(2,1)}, u32[]{:S(2)}, u32[]{:S(2)}) collective-permute-start(bf16[128,128]{1,0:T(8,128)(2,1)} %fusion.13), channel_id=1, source_target_pairs={{0,64},{16,80},{32,96},{48,112},{64,0},{80,16},{96,32},{112,48},{1... | collective-permute-start | bytes 98312 | tf_op jit(solution)/shard_map/ppermute | solution.py:244
  163.2 6.3 %collective-permute-start.10 = (bf16[128,384]{1,0:T(8,128)(2,1)S(1)}, bf16[128,384]{1,0:T(8,128)(2,1)S(1)}, u32[]{:S(2)}, u32[]{:S(2)}) collective-permute-start(bf16[128,384]{1,0:T(8,128)(2,1)S(1)} %get-tuple-element.91), channel_id=1, source_target_pairs={{0,2},{1,3},{2,0},{3,1},{4,6},{5,7},{6,4},{7,5},{8,10},{9,11},{10,... | collective-permute-start | bytes 294920 | tf_op jit(solution)/shard_map/ppermute | solution.py:255
  164.0 6.4 %collective-permute-start.8 = (bf16[128,384]{1,0:T(8,128)(2,1)S(1)}, bf16[128,384]{1,0:T(8,128)(2,1)S(1)}, u32[]{:S(2)}, u32[]{:S(2)}) collective-permute-start(bf16[128,384]{1,0:T(8,128)(2,1)S(1)} %get-tuple-element.90), channel_id=1, source_target_pairs={{0,1},{1,2},{2,3},{3,0},{4,5},{5,6},{6,7},{7,4},{8,9},{9,10},{10,1... | collective-permute-start | bytes 294920 | tf_op jit(solution)/shard_map/ppermute | solution.py:255
  165.3 5.2 %collective-permute-start.9 = (bf16[128,384]{1,0:T(8,128)(2,1)S(1)}, bf16[128,384]{1,0:T(8,128)(2,1)S(1)}, u32[]{:S(2)}, u32[]{:S(2)}) collective-permute-start(bf16[128,384]{1,0:T(8,128)(2,1)S(1)} %get-tuple-element.92), channel_id=1, source_target_pairs={{0,3},{1,0},{2,1},{3,2},{4,7},{5,4},{6,5},{7,6},{8,11},{9,8},{10,9... | collective-permute-start | bytes 294920 | tf_op jit(solution)/shard_map/ppermute | solution.py:255
  170.5 5.2 %collective-permute-start.18 = (bf16[128,512]{1,0:T(8,128)(2,1)S(1)}, bf16[128,512]{1,0:T(8,128)(2,1)S(1)}, u32[]{:S(2)}, u32[]{:S(2)}) collective-permute-start(bf16[128,512]{1,0:T(8,128)(2,1)S(1)} %pad_maximum_fusion.6.refs_0_), channel_id=1, source_target_pairs={{0,3},{1,0},{2,1},{3,2},{4,7},{5,4},{6,5},{7,6},{8,11},{9,8},{10,9... | collective-permute-start | bytes 393224 | tf_op jit(solution)/shard_map/ppermute | solution.py:255
  173.2 6.5 %collective-permute-start.19 = (bf16[128,512]{1,0:T(8,128)(2,1)S(1)}, bf16[128,512]{1,0:T(8,128)(2,1)S(1)}, u32[]{:S(2)}, u32[]{:S(2)}) collective-permute-start(bf16[128,512]{1,0:T(8,128)(2,1)S(1)} %pad_maximum_fusion.6.refs_0_), channel_id=1, source_target_pairs={{0,2},{1,3},{2,0},{3,1},{4,6},{5,7},{6,4},{7,5},{8,10},{9,11},{10,... | collective-permute-start | bytes 393224 | tf_op jit(solution)/shard_map/ppermute | solution.py:255
  174.3 6.8 %collective-permute-start.20 = (bf16[128,512]{1,0:T(8,128)(2,1)S(1)}, bf16[128,512]{1,0:T(8,128)(2,1)S(1)}, u32[]{:S(2)}, u32[]{:S(2)}) collective-permute-start(bf16[128,512]{1,0:T(8,128)(2,1)S(1)} %pad_maximum_fusion.6.refs_0_), channel_id=1, source_target_pairs={{0,1},{1,2},{2,3},{3,0},{4,5},{5,6},{6,7},{7,4},{8,9},{9,10},{10,1... | collective-permute-start | bytes 393224 | tf_op jit(solution)/shard_map/ppermute | solution.py:255
  182.0 12.1 %collective-permute-start.21 = (bf16[512,512]{1,0:T(8,128)(2,1)S(1)}, bf16[512,512]{1,0:T(8,128)(2,1)S(1)}, u32[]{:S(2)}, u32[]{:S(2)}) collective-permute-start(bf16[512,512]{1,0:T(8,128)(2,1)S(1)} %serve.1.refs_0_), channel_id=1, source_target_pairs={{0,48},{16,0},{32,16},{48,32},{64,112},{80,64},{96,80},{112,96},{1... | collective-permute-start | bytes 1572872 | tf_op jit(solution)/shard_map/ppermute | solution.py:208
  185.4 12.7 %collective-permute-start.22 = (bf16[512,512]{1,0:T(8,128)(2,1)S(1)}, bf16[512,512]{1,0:T(8,128)(2,1)S(1)}, u32[]{:S(2)}, u32[]{:S(2)}) collective-permute-start(bf16[512,512]{1,0:T(8,128)(2,1)S(1)} %serve.1.refs_0_), channel_id=1, source_target_pairs={{0,16},{16,32},{32,48},{48,0},{64,80},{80,96},{96,112},{112,64},{1... | collective-permute-start | bytes 1572872 | tf_op jit(solution)/shard_map/ppermute | solution.py:208
  185.4 12.8 %collective-permute-start.23 = (bf16[512,512]{1,0:T(8,128)(2,1)S(1)}, bf16[512,512]{1,0:T(8,128)(2,1)S(1)}, u32[]{:S(2)}, u32[]{:S(2)}) collective-permute-start(bf16[512,512]{1,0:T(8,128)(2,1)S(1)} %serve.1.refs_0_), channel_id=1, source_target_pairs={{0,64},{16,80},{32,96},{48,112},{64,0},{80,16},{96,32},{112,48},{1... | collective-permute-start | bytes 1572872 | tf_op jit(solution)/shard_map/ppermute | solution.py:208
  198.4 13.3 %collective-permute-start.24 = (bf16[512,512]{1,0:T(8,128)(2,1)S(1)}, bf16[512,512]{1,0:T(8,128)(2,1)S(1)}, u32[]{:S(2)}, u32[]{:S(2)}) collective-permute-start(bf16[512,512]{1,0:T(8,128)(2,1)S(1)} %get-tuple-element.95), channel_id=1, source_target_pairs={{0,48},{16,0},{32,16},{48,32},{64,112},{80,64},{96,80},{112,96},{1... | collective-permute-start | bytes 1572872 | tf_op jit(solution)/shard_map/ppermute | solution.py:208
  202.2 10.4 %collective-permute-start.25 = (bf16[512,512]{1,0:T(8,128)(2,1)S(1)}, bf16[512,512]{1,0:T(8,128)(2,1)S(1)}, u32[]{:S(2)}, u32[]{:S(2)}) collective-permute-start(bf16[512,512]{1,0:T(8,128)(2,1)S(1)} %get-tuple-element.94), channel_id=1, source_target_pairs={{0,16},{16,32},{32,48},{48,0},{64,80},{80,96},{96,112},{112,64},{1... | collective-permute-start | bytes 1572872 | tf_op jit(solution)/shard_map/ppermute | solution.py:208
  202.2 13.5 %collective-permute-start.26 = (bf16[512,512]{1,0:T(8,128)(2,1)S(1)}, bf16[512,512]{1,0:T(8,128)(2,1)S(1)}, u32[]{:S(2)}, u32[]{:S(2)}) collective-permute-start(bf16[512,512]{1,0:T(8,128)(2,1)S(1)} %get-tuple-element.93), channel_id=1, source_target_pairs={{0,64},{16,80},{32,96},{48,112},{64,0},{80,16},{96,32},{112,48},{1... | collective-permute-start | bytes 1572872 | tf_op jit(solution)/shard_map/ppermute | solution.py:208
  215.7 7.9 %collective-permute-start.27 = (bf16[256,512]{1,0:T(8,128)(2,1)S(1)}, bf16[256,512]{1,0:T(8,128)(2,1)S(1)}, u32[]{:S(2)}, u32[]{:S(2)}) collective-permute-start(bf16[256,512]{1,0:T(8,128)(2,1)S(1)} %slice.146), channel_id=1, source_target_pairs={{0,48},{16,0},{32,16},{48,32},{64,112},{80,64},{96,80},{112,96},{1... | collective-permute-start | bytes 786440 | tf_op jit(solution)/shard_map/ppermute | solution.py:208
  217.6 8.0 %collective-permute-start.28 = (bf16[256,512]{1,0:T(8,128)(2,1)S(1)}, bf16[256,512]{1,0:T(8,128)(2,1)S(1)}, u32[]{:S(2)}, u32[]{:S(2)}) collective-permute-start(bf16[256,512]{1,0:T(8,128)(2,1)S(1)} %slice.147), channel_id=1, source_target_pairs={{0,64},{16,80},{32,96},{48,112},{64,0},{80,16},{96,32},{112,48},{1... | collective-permute-start | bytes 786440 | tf_op jit(solution)/shard_map/ppermute | solution.py:208
